TPU v7x, 512 devices: a whole 4x8x8 slice. The times are simulated.
512 devices in a mesh: grp: 16 (over y_hi, x, core), blk: 32 (over z, y_lo).
Axes of the slice: x: 4, y: 8 (y_hi: 2, y_lo: 4; y = y_hi * 4 + y_lo), z: 8, core: 2. Of those that a mesh axis runs over, the one named last changes fastest.
Arguments:
- vertex: float32 [16, 32, 1024, 256], P('grp', 'blk'), may hold values from -1.5 to 1.5
- context: float32 [16, 32, 96, 256], P('grp', 'blk'), may hold values from -1.5 to 1.5
- counts: int32 [16, 32, 6, 96, 1024], P('grp', 'blk'), may hold values from 0 to 7
- tile_index: int32 [16, 32, 6], P('grp', 'blk'), may hold values from 0 to 5, each once within a row
- matching: int32 [16], replicated, may hold values from 0 to 15, as said below
Outputs:
- vertex_out: float32 [16, 32, 1024, 256], P('grp', 'blk')
- context_out: float32 [16, 32, 96, 256], P('grp', 'blk')
Inputs may be any that keep to these rules, and one draw needn't show every extreme that they name: matching names every group once. `tile_index`: each row over the last dimension names every stored tile once.
All inputs are finite; a program needn't handle non-finite values.
Results may differ from a plain program's by a relative error of at most 0.00014.
Values sent between devices are 32-bit elements; how exact they have to be, the bound alone decides.
No kernel may reach another device: no remote copies, remote signals or barrier semaphores. Data moves between devices by JAX's collectives and lax.ppermute only.
A program may use at most 64 MiB of HBM per device.

v0:
```python
import jax
import jax.numpy as jnp
from jax import lax
from jax.sharding import PartitionSpec as P

STEPS = 6
FIRST = 4


lr_rate = 0.003


def from_everyone(array, axis):
    devices = lax.axis_size(axis)
    return lax.all_to_all(
        jnp.broadcast_to(array[None], (devices, *array.shape)), axis, 0, 0, tiled=True
    )


def laid_out(parts, dim):
    lengths = list(parts.shape[1:])
    lengths[dim] *= parts.shape[0]
    return jnp.moveaxis(parts, 0, dim).reshape(lengths)


def gathered_copies(array, axis, dim):
    parts = from_everyone(array, axis)
    return laid_out(parts, dim)


def shifted(block, axis, distance):
    devices = range(lax.axis_size(axis))
    route = [((i - distance) % len(devices), i) for i in devices]
    return lax.ppermute(block, axis, route)


def update(vertex_rows, context_rows, weight_tile):
    logits = jnp.dot(
        context_rows,
        vertex_rows.T,
        precision=lax.Precision.HIGHEST,
        preferred_element_type=jnp.float32,
    )
    gradient_logit = (weight_tile + 1.0) * jax.nn.sigmoid(logits) - weight_tile
    vertex_grad = jnp.dot(
        gradient_logit.T,
        context_rows,
        precision=lax.Precision.HIGHEST,
        preferred_element_type=jnp.float32,
    )
    context_grad = jnp.dot(
        gradient_logit,
        vertex_rows,
        precision=lax.Precision.HIGHEST,
        preferred_element_type=jnp.float32,
    )
    return (vertex_rows - lr_rate * vertex_grad, context_rows - lr_rate * context_grad)


def regroup(context_rows, matching):
    own_group = lax.axis_index("grp")
    selected = (matching == own_group).astype(jnp.float32)
    return jnp.einsum(
        "k,krd->rd",
        selected,
        gathered_copies(context_rows[None], "grp", 0),
        precision=lax.Precision.HIGHEST,
    )


def on_device(vertex, context, counts, tile_index, matching):
    vertex_rows = vertex[0, 0]
    context_rows = context[0, 0]
    stored = counts[0, 0]
    order = tile_index[0, 0]
    for step_num in range(STEPS):
        picked = lax.dynamic_index_in_dim(stored, order[step_num], 0, keepdims=False)
        vertex_rows, context_rows = update(vertex_rows, context_rows, picked.astype(jnp.float32))
        if step_num + 1 < STEPS:
            if step_num + 1 == FIRST:
                context_rows = regroup(context_rows, matching)
            else:
                context_rows = shifted(context_rows, "blk", 1)
    return (vertex_rows[None, None], context_rows[None, None])


def solution(mesh):
    in_specs = (
        P("grp", "blk", None, None),
        P("grp", "blk", None, None),
        P("grp", "blk", None, None, None),
        P("grp", "blk", None),
        P(),
    )
    out_specs = (P("grp", "blk", None, None), P("grp", "blk", None, None))
    return jax.shard_map(
        on_device, mesh=mesh, in_specs=in_specs, out_specs=out_specs, check_vma=False
    )
```

profile of v0, /device:TPU:7, one launch (start us, length us, event | category | flops | bytes accessed | tf_op | source)
XLA Modules:
  0.0 117.7 jit_solution(4565959545954593464)
XLA Ops:
  0.6 0.0 copy-start
  0.7 1.5 %fusion.57 = (s32[1,1,1]{2,1,0:T(1,128)}, s32[1,1,1]{2,1,0:T(1,128)}, s32[1,1,1]{2,1,0:T(1,128)}, s32[1,1,1]{2,1,0:T(1,128)}, s32[1,1,1]{2,1,0:T(1,128)}, /*index=5*/s32[1,1,1]{2,1,0:T(1,128)}) fusion(s32[1,1,6]{2,1,0:T(1,128)} %param.8), kind=kLoop, calls=%fused_computation.81 | loop fusion | bytes 48 | tf_op jit(solution)/shard_map/slice | solution.py:77
  4.1 2.5 %fusion.28 = f32[96,1024]{1,0:T(8,128)S(1)} fusion(f32[1,1,1024,256]{3,2,1,0:T(8,128)} %param.5, s32[1,1,6,96,1024]{4,3,2,1,0:T(8,128)} %param.7, s32[]{:T(128)S(6)} %select_n.19, f32[1,1,96,256]{3,2,1,0:T(8,128)} %param.6), kind=kOutput, calls=%fused_computation.40 | convolution fusion | flops 302678016 | bytes 1933316 | tf_op jit(solution)/shard_map/dot_general | solution.py:38
  6.6 1.5 %fusion.45 = f32[96,256]{1,0:T(8,128)S(1)} fusion(f32[96,1024]{1,0:T(8,128)S(1)} %fusion.28, f32[1,1,1024,256]{3,2,1,0:T(8,128)S(1)} %copy-done, f32[1,1,96,256]{3,2,1,0:T(8,128)} %param.6), kind=kOutput, calls=%fused_computation.63 | convolution fusion | flops 302039040 | bytes 1638400 | tf_op jit(solution)/shard_map/dot_general | solution.py:51
  8.1 3.2 %collective-permute-start = (f32[96,256]{1,0:T(8,128)S(1)}, f32[96,256]{1,0:T(8,128)S(1)}, u32[]{:S(2)}, u32[]{:S(2)}) collective-permute-start(f32[96,256]{1,0:T(8,128)S(1)} %fusion.45), channel_id=1, source_target_pairs={{31,0},{0,1},{1,2},{2,3},{3,4},{4,5},{5,6},{6,7},{7,8},{8,9},{9,10... | collective-permute-start | bytes 294920 | tf_op jit(solution)/shard_map/ppermute | solution.py:34
  11.4 1.0 fusion.8
  18.1 6.2 %collective-permute-done = f32[96,256]{1,0:T(8,128)S(1)} collective-permute-done((f32[96,256]{1,0:T(8,128)S(1)}, f32[96,256]{1,0:T(8,128)S(1)}, u32[]{:S(2)}, u32[]{:S(2)}) %collective-permute-start) | collective-permute-done | bytes 98336 | tf_op jit(solution)/shard_map/ppermute | solution.py:34
  24.3 2.2 %fusion.30 = f32[96,1024]{1,0:T(8,128)S(1)} fusion(f32[96,256]{1,0:T(8,128)S(1)} %collective-permute-done, f32[1024,256]{1,0:T(8,128)S(1)} %fusion.8, s32[1,1,6,96,1024]{4,3,2,1,0:T(8,128)} %param.7, s32[]{:T(128)S(6)} %select_n.20), kind=kOutput, calls=%fused_computation.42 | convolution fusion | flops 302678016 | bytes 1933316 | tf_op jit(solution)/shard_map/dot_general | solution.py:38
  26.5 0.7 fusion.44
  27.2 1.9 %collective-permute-start.1 = (f32[96,256]{1,0:T(8,128)S(1)}, f32[96,256]{1,0:T(8,128)S(1)}, u32[]{:S(2)}, u32[]{:S(2)}) collective-permute-start(f32[96,256]{1,0:T(8,128)S(1)} %fusion.44), channel_id=1, source_target_pairs={{31,0},{0,1},{1,2},{2,3},{3,4},{4,5},{5,6},{6,7},{7,8},{8,9},{9,10... | collective-permute-start | bytes 294920 | tf_op jit(solution)/shard_map/ppermute | solution.py:34
  29.1 1.0 fusion.7
  30.1 6.3 %collective-permute-done.1 = f32[96,256]{1,0:T(8,128)S(1)} collective-permute-done((f32[96,256]{1,0:T(8,128)S(1)}, f32[96,256]{1,0:T(8,128)S(1)}, u32[]{:S(2)}, u32[]{:S(2)}) %collective-permute-start.1) | collective-permute-done | bytes 98336 | tf_op jit(solution)/shard_map/ppermute | solution.py:34
  36.4 2.2 %fusion.32 = f32[96,1024]{1,0:T(8,128)S(1)} fusion(f32[96,256]{1,0:T(8,128)S(1)} %collective-permute-done.1, f32[1024,256]{1,0:T(8,128)S(1)} %fusion.7, s32[1,1,6,96,1024]{4,3,2,1,0:T(8,128)} %param.7, s32[]{:T(128)S(6)} %select_n.21), kind=kOutput, calls=%fused_computation.44 | convolution fusion | flops 302678016 | bytes 1933316 | tf_op jit(solution)/shard_map/dot_general | solution.py:38
  38.6 0.6 fusion.43
  39.3 1.9 %collective-permute-start.2 = (f32[96,256]{1,0:T(8,128)S(1)}, f32[96,256]{1,0:T(8,128)S(1)}, u32[]{:S(2)}, u32[]{:S(2)}) collective-permute-start(f32[96,256]{1,0:T(8,128)S(1)} %fusion.43), channel_id=1, source_target_pairs={{31,0},{0,1},{1,2},{2,3},{3,4},{4,5},{5,6},{6,7},{7,8},{8,9},{9,10... | collective-permute-start | bytes 294920 | tf_op jit(solution)/shard_map/ppermute | solution.py:34
  41.2 1.0 fusion.6
  42.2 6.3 %collective-permute-done.2 = f32[96,256]{1,0:T(8,128)S(1)} collective-permute-done((f32[96,256]{1,0:T(8,128)S(1)}, f32[96,256]{1,0:T(8,128)S(1)}, u32[]{:S(2)}, u32[]{:S(2)}) %collective-permute-start.2) | collective-permute-done | bytes 98336 | tf_op jit(solution)/shard_map/ppermute | solution.py:34
  48.5 2.2 %fusion.34 = f32[96,1024]{1,0:T(8,128)S(1)} fusion(f32[96,256]{1,0:T(8,128)S(1)} %collective-permute-done.2, f32[1024,256]{1,0:T(8,128)S(1)} %fusion.6, s32[1,1,6,96,1024]{4,3,2,1,0:T(8,128)} %param.7, s32[]{:T(128)S(6)} %select_n.22), kind=kOutput, calls=%fused_computation.46 | convolution fusion | flops 302678016 | bytes 1933316 | tf_op jit(solution)/shard_map/dot_general | solution.py:38
  50.7 0.6 fusion.42
  51.4 1.3 %broadcast_in_dim.11 = f32[16,1,96,256]{3,2,1,0:T(8,128)} broadcast(f32[96,256]{1,0:T(8,128)S(1)} %fusion.42), dimensions={2,3} | broadcast | bytes 1671168 | tf_op jit(solution)/shard_map/broadcast_in_dim | solution.py:16
  52.7 10.6 %all-to-all-start = ((f32[16,1,96,256]{3,2,1,0:T(8,128)}), f32[16,1,96,256]{3,2,1,0:T(8,128)}, u32[]{:S(2)}, u32[]{:S(2)}) async-start(f32[16,1,96,256]{3,2,1,0:T(8,128)} %broadcast_in_dim.11), calls=%async_computation | async-start | bytes 3145728 | tf_op jit(solution)/shard_map/all_to_all | solution.py:15
  67.1 1.0 fusion.5
  68.2 27.0 %all-to-all-done = f32[16,1,96,256]{3,2,1,0:T(8,128)} async-done(((f32[16,1,96,256]{3,2,1,0:T(8,128)}), f32[16,1,96,256]{3,2,1,0:T(8,128)}, u32[]{:S(2)}, u32[]{:S(2)}) %all-to-all-start) | async-done | bytes 1572896 | tf_op jit(solution)/shard_map/all_to_all | solution.py:15
  95.2 2.8 %fusion = f32[1,96,256]{2,0,1:T(1,128)S(1)} fusion(f32[16,96,256]{2,1,0:T(8,128)} %bitcast.13, s32[16]{0:T(128)S(1)} %copy-done.2, s32[]{:T(128)S(6)} %axis_index.15), kind=kOutput, calls=%fused_computation | convolution fusion | flops 4718608 | bytes 1671236 | tf_op jit(solution)/shard_map/k,krd->rd/dot_general | solution.py:63
  98.1 2.2 %fusion.36 = f32[96,1024]{1,0:T(8,128)S(1)} fusion(f32[1024,256]{1,0:T(8,128)S(1)} %fusion.5, s32[1,1,6,96,1024]{4,3,2,1,0:T(8,128)} %param.7, s32[]{:T(128)S(6)} %select_n.23, f32[1,96,256]{2,0,1:T(1,128)S(1)} %fusion), kind=kOutput, calls=%fused_computation.48 | convolution fusion | flops 302678016 | bytes 1933316 | tf_op jit(solution)/shard_map/dot_general | solution.py:38
  100.3 0.6 fusion.41
  100.9 6.1 %collective-permute-start.3 = (f32[96,256]{1,0:T(8,128)S(1)}, f32[96,256]{1,0:T(8,128)S(1)}, u32[]{:S(2)}, u32[]{:S(2)}) collective-permute-start(f32[96,256]{1,0:T(8,128)S(1)} %fusion.41), channel_id=1, source_target_pairs={{31,0},{0,1},{1,2},{2,3},{3,4},{4,5},{5,6},{6,7},{7,8},{8,9},{9,10... | collective-permute-start | bytes 294920 | tf_op jit(solution)/shard_map/ppermute | solution.py:34
  107.0 1.0 fusion.4
  108.0 4.2 %collective-permute-done.3 = f32[96,256]{1,0:T(8,128)S(1)} collective-permute-done((f32[96,256]{1,0:T(8,128)S(1)}, f32[96,256]{1,0:T(8,128)S(1)}, u32[]{:S(2)}, u32[]{:S(2)}) %collective-permute-start.3) | collective-permute-done | bytes 98336 | tf_op jit(solution)/shard_map/ppermute | solution.py:34
  112.2 2.2 %fusion.38 = f32[96,1024]{1,0:T(8,128)S(1)} fusion(f32[96,256]{1,0:T(8,128)S(1)} %collective-permute-done.3, f32[1024,256]{1,0:T(8,128)S(1)} %fusion.4, s32[1,1,6,96,1024]{4,3,2,1,0:T(8,128)} %param.7, s32[]{:T(128)S(6)} %select_n.24), kind=kOutput, calls=%fused_computation.50 | convolution fusion | flops 302678016 | bytes 1933316 | tf_op jit(solution)/shard_map/dot_general | solution.py:38
  114.4 2.0 %fusion.3 = f32[1,1,1024,256]{3,2,1,0:T(8,128)} fusion(f32[1024,256]{1,0:T(8,128)S(1)} %fusion.4, f32[96,1024]{1,0:T(8,128)S(1)} %fusion.38, f32[96,256]{1,0:T(8,128)S(1)} %collective-permute-done.3), kind=kOutput, calls=%fused_computation.4 | convolution fusion | flops 302514176 | bytes 2588672 | tf_op jit(solution)/shard_map/dot_general | solution.py:45
  116.4 1.3 %fusion.40 = f32[1,1,96,256]{3,2,1,0:T(8,128)} fusion(f32[96,256]{1,0:T(8,128)S(1)} %collective-permute-done.3, f32[96,1024]{1,0:T(8,128)S(1)} %fusion.38, f32[1024,256]{1,0:T(8,128)S(1)} %fusion.4), kind=kOutput, calls=%fused_computation.53 | convolution fusion | flops 302039040 | bytes 1638400 | tf_op jit(solution)/shard_map/dot_general | solution.py:51
  (5 shorter events, 0.0 us)
Async XLA Ops:
  0.6 5.9 %copy-start = (f32[1,1,1024,256]{3,2,1,0:T(8,128)S(1)}, f32[1,1,1024,256]{3,2,1,0:T(8,128)}, u32[]{:S(2)}) copy-start(f32[1,1,1024,256]{3,2,1,0:T(8,128)} %param.5) | copy-start | bytes 3145732
  0.6 10.7 %copy-start.1 = (f32[1,1,96,256]{3,2,1,0:T(8,128)S(1)}, f32[1,1,96,256]{3,2,1,0:T(8,128)}, u32[]{:S(2)}) copy-start(f32[1,1,96,256]{3,2,1,0:T(8,128)} %param.6) | copy-start | bytes 294916
  8.1 16.2 %collective-permute-start = (f32[96,256]{1,0:T(8,128)S(1)}, f32[96,256]{1,0:T(8,128)S(1)}, u32[]{:S(2)}, u32[]{:S(2)}) collective-permute-start(f32[96,256]{1,0:T(8,128)S(1)} %fusion.45), channel_id=1, source_target_pairs={{31,0},{0,1},{1,2},{2,3},{3,4},{4,5},{5,6},{6,7},{7,8},{8,9},{9,10... | collective-permute-start | bytes 294920 | tf_op jit(solution)/shard_map/ppermute | solution.py:34
  27.2 9.3 %collective-permute-start.1 = (f32[96,256]{1,0:T(8,128)S(1)}, f32[96,256]{1,0:T(8,128)S(1)}, u32[]{:S(2)}, u32[]{:S(2)}) collective-permute-start(f32[96,256]{1,0:T(8,128)S(1)} %fusion.44), channel_id=1, source_target_pairs={{31,0},{0,1},{1,2},{2,3},{3,4},{4,5},{5,6},{6,7},{7,8},{8,9},{9,10... | collective-permute-start | bytes 294920 | tf_op jit(solution)/shard_map/ppermute | solution.py:34
  39.3 9.3 %collective-permute-start.2 = (f32[96,256]{1,0:T(8,128)S(1)}, f32[96,256]{1,0:T(8,128)S(1)}, u32[]{:S(2)}, u32[]{:S(2)}) collective-permute-start(f32[96,256]{1,0:T(8,128)S(1)} %fusion.43), channel_id=1, source_target_pairs={{31,0},{0,1},{1,2},{2,3},{3,4},{4,5},{5,6},{6,7},{7,8},{8,9},{9,10... | collective-permute-start | bytes 294920 | tf_op jit(solution)/shard_map/ppermute | solution.py:34
  52.7 42.6 %copy-start.2 = (s32[16]{0:T(128)S(1)}, s32[16]{0:T(128)}, u32[]{:S(2)}) copy-start(s32[16]{0:T(128)} %param.9) | copy-start | bytes 196
  52.7 42.6 %all-to-all-start = ((f32[16,1,96,256]{3,2,1,0:T(8,128)}), f32[16,1,96,256]{3,2,1,0:T(8,128)}, u32[]{:S(2)}, u32[]{:S(2)}) async-start(f32[16,1,96,256]{3,2,1,0:T(8,128)} %broadcast_in_dim.11), calls=%async_computation | async-start | bytes 3145728 | tf_op jit(solution)/shard_map/all_to_all | solution.py:15
  100.9 11.3 %collective-permute-start.3 = (f32[96,256]{1,0:T(8,128)S(1)}, f32[96,256]{1,0:T(8,128)S(1)}, u32[]{:S(2)}, u32[]{:S(2)}) collective-permute-start(f32[96,256]{1,0:T(8,128)S(1)} %fusion.41), channel_id=1, source_target_pairs={{31,0},{0,1},{1,2},{2,3},{3,4},{4,5},{5,6},{6,7},{7,8},{8,9},{9,10... | collective-permute-start | bytes 294920 | tf_op jit(solution)/shard_map/ppermute | solution.py:34
where the time goes:
time: 118 us
  waiting for transfers between devices  50.1 us (42%)
  matrix products  28.8 us (24%)
  starting transfers between devices  23.8 us (20%)
  between operations  12.2 us (10%)
  local copies, waits for them, and re-layouts  2.86 us (2%)
    all_to_all x1, waiting for transfers between devices, from_everyone(): lax.all_to_all(jnp.broadcast_to(array[None], (devices, *array.shape)), ax...  27 us
    ppermute x4, waiting for transfers between devices, shifted(): return lax.ppermute(block, axis, route)  23 us
    dot_general x6, matrix products, update(): jnp.dot(context_rows, vertex_rows.T, precision=lax.Precision.HIGHEST, pre...  13.4 us
    ppermute x4, starting transfers between devices, shifted(): return lax.ppermute(block, axis, route)  13.1 us
    all_to_all x1, starting transfers between devices, from_everyone(): lax.all_to_all(jnp.broadcast_to(array[None], (devices, *array.shape)), ax...  10.6 us
    dot_general x6, matrix products, update(): jnp.dot(gradient_logit.T, context_rows, precision=lax.Precision.HIGHEST,...  7.13 us
    dot_general x6, matrix products, update(): jnp.dot(gradient_logit, vertex_rows, precision=lax.Precision.HIGHEST, pre...  5.44 us
    dot_general x1, matrix products, regroup(): jnp.einsum('k,krd->rd', selected, gathered_copies(context_rows[None], 'gr...  2.84 us
  transfers between devices with their start and end apart: 5, of which 5 were waited for; matrix products, arithmetic and copies ran while one was open for 4% of the time, Pallas kernels for 0%

commit v1 on v0

v1 whole, which is shorter than its diff:
```python
import functools

import jax
import jax.numpy as jnp
from jax import lax
from jax.experimental import pallas as pl
from jax.experimental.pallas import tpu as pltpu
from jax.sharding import PartitionSpec as P

STEPS = 6
FIRST = 4
CR, VR, D = 96, 1024, 256
N_X, N_CORE = 4, 2
N_GRP = 16
lr_rate = 0.003

F32, BF16 = jnp.float32, jnp.bfloat16
CHUNK = 256
PARTS = VR // CHUNK
VMEM = pl.BlockSpec(memory_space=pltpu.VMEM)
SMEM = pl.BlockSpec(memory_space=pltpu.SMEM)
HBM = pl.BlockSpec(memory_space=pltpu.HBM)


def array(shape, dtype=F32):
    return jax.ShapeDtypeStruct(shape, dtype)


def call(kernel, name, out_shape, in_specs, out_specs, flops, moved, scratch=()):
    return pl.pallas_call(
        kernel,
        out_shape=out_shape,
        in_specs=in_specs,
        out_specs=out_specs,
        scratch_shapes=scratch,
        name=name,
        cost_estimate=pl.CostEstimate(flops=flops, bytes_accessed=moved, transcendentals=CR * VR),
        compiler_params=pltpu.CompilerParams(vmem_limit_bytes=16 * 1024 * 1024),
    )


def halves(x):
    high = x.astype(BF16)
    return high, (x - high.astype(F32)).astype(BF16)


def product(a, b, a_dim, b_dim):
    return lax.dot_general(a, b, (((a_dim,), (b_dim,)), ((), ())), preferred_element_type=F32)


def logit_gradient(ch, cc, high, low, weight):
    both = product(cc, high, 1, 1)
    logits = both[:CR] + (both[CR:] + product(ch, low, 1, 1))
    weight = weight.astype(F32)
    return (weight + 1.0) * jax.nn.sigmoid(logits) - weight


def context_part(rh, rl, high, low):
    both = product(jnp.concatenate([rh, rl], 0), high, 0 + 1, 0)
    return both[:CR] + (both[CR:] + product(rh, low, 1, 0))


def vertex_part(rh, rl, double, cl):
    return product(jnp.concatenate([rh, rl], 0), double, 0, 0) + product(rh, cl, 0, 0)


def rows_of(part):
    return pl.ds(part * CHUNK, CHUNK)


def first_kernel(order, vertex, context, counts, c_out, r_out, c_in, u_out, tile, sems):
    copies = [
        pltpu.make_async_copy(context.at[0, 0], c_in, sems.at[0]),
        pltpu.make_async_copy(counts.at[0, 0, order[0, 0, 0]], tile, sems.at[1]),
    ]
    for part in range(PARTS):
        rows = rows_of(part)
        copies.append(
            pltpu.make_async_copy(vertex.at[0, 0, rows, :], u_out.at[rows, :], sems.at[2 + part])
        )
    for copy in copies:
        copy.start()
    copies[0].wait()
    copies[1].wait()
    c = c_in[...]
    ch, cl = halves(c)
    cc = jnp.concatenate([ch, cl], 0)
    total = jnp.zeros((CR, D), F32)
    for part in range(PARTS):
        rows = rows_of(part)
        copies[2 + part].wait()
        high, low = halves(u_out[rows, :])
        r = logit_gradient(ch, cc, high, low, tile[:, rows])
        r_out[:, rows] = r
        total = total + context_part(*halves(r), high, low)
    c_out[...] = c - lr_rate * total


def context_kernel(c_in, high_in, low_in, tile, c_out, r_out):
    c = c_in[...]
    ch, cl = halves(c)
    cc = jnp.concatenate([ch, cl], 0)
    total = jnp.zeros((CR, D), F32)
    for part in range(PARTS):
        rows = rows_of(part)
        high, low = high_in[rows, :], low_in[rows, :]
        r = logit_gradient(ch, cc, high, low, tile[:, rows])
        r_out[:, rows] = r
        total = total + context_part(*halves(r), high, low)
    c_out[...] = c - lr_rate * total


def source_group(matching, group):
    source = jnp.int32(0)
    for k in range(N_GRP):
        source = jnp.where(matching[k] == group, jnp.int32(k), source)
    return source


def x_of(group):
    return (group // N_CORE) % N_X


def pack_kernel(matching, own, held, out):
    group = own[0]
    base = group - x_of(group) * N_CORE
    for x in range(N_X):
        source = source_group(matching, base + x * N_CORE)
        out[x] = held[(source // (N_X * N_CORE)) * N_CORE + source % N_CORE]


def received_kernel(matching, own, received, u_in, tile, c_out, r_out, c_in):
    c = received[x_of(source_group(matching, own[0]))]
    c_in[...] = c
    ch, cl = halves(c)
    cc = jnp.concatenate([ch, cl], 0)
    total = jnp.zeros((CR, D), F32)
    for part in range(PARTS):
        rows = rows_of(part)
        high, low = halves(u_in[rows, :])
        r = logit_gradient(ch, cc, high, low, tile[:, rows])
        r_out[:, rows] = r
        total = total + context_part(*halves(r), high, low)
    c_out[...] = c - lr_rate * total


def vertex_kernel(order, u_in, r_in, c_in, counts, u_out, tile, *rest, step):
    *halves_out, sem = rest
    copy = pltpu.make_async_copy(counts.at[0, 0, order[0, 0, step]], tile, sem)
    copy.start()
    ch, cl = halves(c_in[...])
    double = jnp.concatenate([ch, ch], 0)
    for part in range(PARTS):
        rows = rows_of(part)
        u = u_in[rows, :] - lr_rate * vertex_part(*halves(r_in[:, rows]), double, cl)
        u_out[rows, :] = u
        for half_out, half in zip(halves_out, halves(u)):
            half_out[rows, :] = half
    copy.wait()


def last_kernel(u_in, c_ref, high_in, low_in, tile, vertex_out, context_out, u_new, c_new, sems):
    c = c_ref[...]
    ch, cl = halves(c)
    cc = jnp.concatenate([ch, cl], 0)
    double = jnp.concatenate([ch, ch], 0)
    total = jnp.zeros((CR, D), F32)
    copies = []
    for part in range(PARTS):
        rows = rows_of(part)
        high, low = high_in[rows, :], low_in[rows, :]
        rh, rl = halves(logit_gradient(ch, cc, high, low, tile[:, rows]))
        u_new[rows, :] = u_in[rows, :] - lr_rate * vertex_part(rh, rl, double, cl)
        copies.append(
            pltpu.make_async_copy(u_new.at[rows, :], vertex_out.at[0, 0, rows, :], sems.at[part])
        )
        copies[-1].start()
        total = total + context_part(rh, rl, high, low)
    c_new[...] = c - lr_rate * total
    copies.append(pltpu.make_async_copy(c_new, context_out.at[0, 0], sems.at[PARTS]))
    copies[-1].start()
    for copy in copies:
        copy.wait()


MATMUL = 6 * CR * VR * D
BLOCK = 4 * CR * D
GRADIENT = 4 * CR * VR
VERTEX = 4 * VR * D

UPDATED = (array((CR, D)), array((CR, VR)), array((CR, D)))


def first_step(order, vertex, context, counts):
    return call(
        first_kernel,
        "first_step",
        UPDATED + (array((VR, D)),),
        [SMEM, HBM, HBM, HBM],
        (VMEM,) * 4,
        2 * MATMUL,
        2 * VERTEX,
        [pltpu.VMEM((CR, VR), jnp.int32), pltpu.SemaphoreType.DMA((2 + PARTS,))],
    )(order, vertex, context, counts)


def context_step(c, high, low, tile):
    return call(
        context_kernel,
        "context_step",
        UPDATED[:2],
        [VMEM] * 4,
        (VMEM,) * 2,
        2 * MATMUL,
        VERTEX,
    )(c, high, low, tile)


def received_step(matching, own, received, u, tile):
    return call(
        received_kernel,
        "received_step",
        UPDATED,
        [SMEM] * 2 + [VMEM] * 3,
        (VMEM,) * 3,
        2 * MATMUL,
        VERTEX,
    )(matching, own, received, u, tile)


def vertex_step(order, u, r, c, counts, step):
    outs = (array((VR, D)), array((CR, VR), jnp.int32))
    if step != FIRST:
        outs += (array((VR, D), BF16),) * 2
    return call(
        functools.partial(vertex_kernel, step=step),
        "vertex_step",
        outs,
        [SMEM, VMEM, VMEM, VMEM, HBM],
        (VMEM,) * len(outs),
        MATMUL,
        4 * VERTEX,
        [pltpu.SemaphoreType.DMA],
    )(order, u, r, c, counts)


def last_step(u, c, high, low, tile):
    return call(
        last_kernel,
        "last_step",
        (array((1, 1, VR, D)), array((1, 1, CR, D))),
        [VMEM] * 5,
        (HBM, HBM),
        3 * MATMUL,
        2 * VERTEX,
        [
            pltpu.VMEM((VR, D), F32),
            pltpu.VMEM((CR, D), F32),
            pltpu.SemaphoreType.DMA((PARTS + 1,)),
        ],
    )(u, c, high, low, tile)


def pack(matching, own, held):
    return call(
        pack_kernel,
        "pack",
        array((N_X, CR, D)),
        [SMEM, SMEM, VMEM],
        VMEM,
        0,
        8 * BLOCK,
    )(matching, own, held)


def shifted(block):
    devices = lax.axis_size("blk")
    return lax.ppermute(block, "blk", [(i, (i + 1) % devices) for i in range(devices)])


def on_device(vertex, context, counts, tile_index, matching):
    own = lax.axis_index("grp").astype(jnp.int32).reshape(1)
    vertex, context, counts = (
        pltpu.with_memory_space_constraint(x, pltpu.HBM) for x in (vertex, context, counts)
    )
    half = N_X * N_CORE
    columns = [[g, g + 1, g + half, g + half + 1] for g in range(0, half, N_CORE)]
    rings = [[y * half + x * N_CORE + k for x in range(N_X)] for y in range(2) for k in range(N_CORE)]
    c_new, r, c, u = first_step(tile_index, vertex, context, counts)
    for step in range(1, STEPS):
        if step == FIRST:
            held = lax.all_gather(c_new, "grp", axis_index_groups=columns)
            sent = pack(matching, own, held)
            moved = lax.all_to_all(sent, "grp", 0, 0, axis_index_groups=rings, tiled=True)
        else:
            moved = shifted(c_new)
        u, tile, *split = vertex_step(tile_index, u, r, c, counts, step)
        if step == STEPS - 1:
            return last_step(u, moved, *split, tile)
        if step == FIRST:
            c_new, r, c = received_step(matching, own, moved, u, tile)
        else:
            c = moved
            c_new, r = context_step(c, *split, tile)


def solution(mesh):
    in_specs = (
        P("grp", "blk", None, None),
        P("grp", "blk", None, None),
        P("grp", "blk", None, None, None),
        P("grp", "blk", None),
        P(),
    )
    out_specs = (P("grp", "blk", None, None), P("grp", "blk", None, None))
    return jax.shard_map(
        on_device, mesh=mesh, in_specs=in_specs, out_specs=out_specs, check_vma=False
    )
```

time: 118 us -> 83.1 us (0.70)
  the two profiles are of different devices: /device:TPU:7 before, /device:TPU:2 now
where the time goes in v1:
time: 83.1 us; the launch traced here: 82.6 us
  waiting for transfers between devices  37.3 us (45%)
  Pallas kernels  19.7 us (24%)
  starting transfers between devices  14.1 us (17%)
  blocking collectives  10 us (12%)
    ppermute x4, waiting for transfers between devices, shifted(): lax.ppermute(block, 'blk', [(i, (i + 1) % devices) for i in range(devices)])  31.9 us
    all_gather x1, blocking collectives, on_device(): held = lax.all_gather(c_new, 'grp', axis_index_groups=columns)  10 us
    ppermute x4, starting transfers between devices, shifted(): lax.ppermute(block, 'blk', [(i, (i + 1) % devices) for i in range(devices)])  9.25 us
    pallas_call x5, Pallas kernels, vertex_step(): call(functools.partial(vertex_kernel, step=step), 'vertex_step', outs, [S...  8.53 us
    all_to_all x1, waiting for transfers between devices, on_device(): lax.all_to_all(sent, 'grp', 0, 0, axis_index_groups=rings, tiled=True)  5.41 us
    all_to_all x1, starting transfers between devices, on_device(): lax.all_to_all(sent, 'grp', 0, 0, axis_index_groups=rings, tiled=True)  4.82 us
    pallas_call x1, Pallas kernels, first_step(): call(first_kernel, 'first_step', UPDATED + (array((VR, D)),), [SMEM, HBM,...  3.31 us
    pallas_call x3, Pallas kernels, context_step(): call(context_kernel, 'context_step', UPDATED[:2], [VMEM] * 4, (VMEM,) * 2...  2.85 us
  transfers between devices with their start and end apart: 5, of which 5 were waited for; matrix products, arithmetic and copies ran while one was open for 0% of the time, Pallas kernels for 10%

profile of v1, /device:TPU:2, one launch (start us, length us, event | category | flops | bytes accessed | tf_op | source)
XLA Modules:
  0.0 82.6 jit_solution(2736825676706663145)
XLA Ops:
  0.6 0.0 copy-start
  0.6 0.6 copy-done
  1.3 3.3 %first_step.1 = (f32[96,256]{1,0:T(8,128)S(1)}, f32[96,1024]{1,0:T(8,128)S(1)}, f32[96,256]{1,0:T(8,128)S(1)}, f32[1024,256]{1,0:T(8,128)S(1)}) custom-call(s32[1,1,6]{2,1,0:T(1,128)S(1)} %copy-done, f32[1,1,1024,256]{3,2,1,0:T(8,128)} %vertex.1, f32[1,1,96,256]{3,2,1,0:T(8,128)} %context.1, s32[1,1,6,96,1024]{4,3,2,1,0:T(8,128)} %counts.11), custom_call_target="tpu_custom_call" | custom-call | flops 301989888 | bytes 2097152 | tf_op jit(solution)/shard_map/first_step/pallas_call | solution.py:195
  4.6 3.5 %collective-permute-start = (f32[96,256]{1,0:T(8,128)S(1)}, f32[96,256]{1,0:T(8,128)S(1)}, u32[]{:S(2)}, u32[]{:S(2)}) collective-permute-start(f32[96,256]{1,0:T(8,128)S(1)} %get-tuple-element.37), channel_id=1, source_target_pairs={{0,1},{1,2},{2,3},{3,4},{4,5},{5,6},{6,7},{7,8},{8,9},{9,10},{10,1... | collective-permute-start | bytes 294920 | tf_op jit(solution)/shard_map/ppermute | solution.py:278
  8.1 1.7 %vertex_step.5 = (f32[1024,256]{1,0:T(8,128)S(1)}, s32[96,1024]{1,0:T(8,128)S(1)}, bf16[1024,256]{1,0:T(8,128)(2,1)S(1)}, bf16[1024,256]{1,0:T(8,128)(2,1)S(1)}) custom-call(s32[1,1,6]{2,1,0:T(1,128)S(1)} %copy-done, f32[1024,256]{1,0:T(8,128)S(1)} %get-tuple-element.33.u_in, f32[96,1024]{1,0:T(8,128)S(1)} %get-tuple-element.34.r_in, ...), custom_call_target="tpu_custom_call" | custom-call | flops 150994944 | bytes 4194304 | tf_op jit(solution)/shard_map/vertex_step/pallas_call | solution.py:235
  9.8 11.6 %collective-permute-done.c_in = f32[96,256]{1,0:T(8,128)S(1)} collective-permute-done((f32[96,256]{1,0:T(8,128)S(1)}, f32[96,256]{1,0:T(8,128)S(1)}, u32[]{:S(2)}, u32[]{:S(2)}) %collective-permute-start) | collective-permute-done | bytes 98336 | tf_op jit(solution)/shard_map/ppermute | solution.py:278
  21.4 1.0 %context_step.3 = (f32[96,256]{1,0:T(8,128)S(1)}, f32[96,1024]{1,0:T(8,128)S(1)}) custom-call(f32[96,256]{1,0:T(8,128)S(1)} %collective-permute-done.c_in, bf16[1024,256]{1,0:T(8,128)(2,1)S(1)} %get-tuple-element.38.high_in, bf16[1024,256]{1,0:T(8,128)(2,1)S(1)} %get-tuple-element.39.low_in, s32[96,1024]{1,0:T(8,128)S(1)} %get-tuple-element.40.tile), custom_call_target="tpu_custom_call" | custom-call | flops 301989888 | bytes 1048576 | tf_op jit(solution)/shard_map/context_step/pallas_call | solution.py:208
  22.3 1.9 %collective-permute-start.1 = (f32[96,256]{1,0:T(8,128)S(1)}, f32[96,256]{1,0:T(8,128)S(1)}, u32[]{:S(2)}, u32[]{:S(2)}) collective-permute-start(f32[96,256]{1,0:T(8,128)S(1)} %get-tuple-element.43), channel_id=1, source_target_pairs={{0,1},{1,2},{2,3},{3,4},{4,5},{5,6},{6,7},{7,8},{8,9},{9,10},{10,1... | collective-permute-start | bytes 294920 | tf_op jit(solution)/shard_map/ppermute | solution.py:278
  24.3 0.0 copy-start.1
  24.3 1.7 %vertex_step.6 = (f32[1024,256]{1,0:T(8,128)S(1)}, s32[96,1024]{1,0:T(8,128)S(1)}, bf16[1024,256]{1,0:T(8,128)(2,1)S(1)}, bf16[1024,256]{1,0:T(8,128)(2,1)S(1)}) custom-call(s32[1,1,6]{2,1,0:T(1,128)S(1)} %copy-done, f32[1024,256]{1,0:T(8,128)S(1)} %get-tuple-element.36.u_in, f32[96,1024]{1,0:T(8,128)S(1)} %get-tuple-element.41.r_in, ...), custom_call_target="tpu_custom_call" | custom-call | flops 150994944 | bytes 4194304 | tf_op jit(solution)/shard_map/vertex_step/pallas_call | solution.py:235
  26.0 6.8 %collective-permute-done.1.c_in = f32[96,256]{1,0:T(8,128)S(1)} collective-permute-done((f32[96,256]{1,0:T(8,128)S(1)}, f32[96,256]{1,0:T(8,128)S(1)}, u32[]{:S(2)}, u32[]{:S(2)}) %collective-permute-start.1) | collective-permute-done | bytes 98336 | tf_op jit(solution)/shard_map/ppermute | solution.py:278
  32.8 0.9 %context_step.4 = (f32[96,256]{1,0:T(8,128)S(1)}, f32[96,1024]{1,0:T(8,128)S(1)}) custom-call(f32[96,256]{1,0:T(8,128)S(1)} %collective-permute-done.1.c_in, bf16[1024,256]{1,0:T(8,128)(2,1)S(1)} %get-tuple-element.44.high_in, bf16[1024,256]{1,0:T(8,128)(2,1)S(1)} %get-tuple-element.45.low_in, s32[96,1024]{1,0:T(8,128)S(1)} %get-tuple-element.46.tile), custom_call_target="tpu_custom_call" | custom-call | flops 301989888 | bytes 1048576 | tf_op jit(solution)/shard_map/context_step/pallas_call | solution.py:208
  33.7 1.9 %collective-permute-start.2 = (f32[96,256]{1,0:T(8,128)S(1)}, f32[96,256]{1,0:T(8,128)S(1)}, u32[]{:S(2)}, u32[]{:S(2)}) collective-permute-start(f32[96,256]{1,0:T(8,128)S(1)} %get-tuple-element.49), channel_id=1, source_target_pairs={{0,1},{1,2},{2,3},{3,4},{4,5},{5,6},{6,7},{7,8},{8,9},{9,10},{10,1... | collective-permute-start | bytes 294920 | tf_op jit(solution)/shard_map/ppermute | solution.py:278
  35.6 0.0 copy-done.1
  35.7 0.0 copy-start.2
  35.7 1.7 %vertex_step.7 = (f32[1024,256]{1,0:T(8,128)S(1)}, s32[96,1024]{1,0:T(8,128)S(1)}, bf16[1024,256]{1,0:T(8,128)(2,1)S(1)}, bf16[1024,256]{1,0:T(8,128)(2,1)S(1)}) custom-call(s32[1,1,6]{2,1,0:T(1,128)S(1)} %copy-done.1, f32[1024,256]{1,0:T(8,128)S(1)} %get-tuple-element.42.u_in, f32[96,1024]{1,0:T(8,128)S(1)} %get-tuple-element.47.r_in, ...), custom_call_target="tpu_custom_call" | custom-call | flops 150994944 | bytes 4194304 | tf_op jit(solution)/shard_map/vertex_step/pallas_call | solution.py:235
  37.4 6.7 %collective-permute-done.2.c_in = f32[96,256]{1,0:T(8,128)S(1)} collective-permute-done((f32[96,256]{1,0:T(8,128)S(1)}, f32[96,256]{1,0:T(8,128)S(1)}, u32[]{:S(2)}, u32[]{:S(2)}) %collective-permute-start.2) | collective-permute-done | bytes 98336 | tf_op jit(solution)/shard_map/ppermute | solution.py:278
  44.1 0.9 %context_step.5 = (f32[96,256]{1,0:T(8,128)S(1)}, f32[96,1024]{1,0:T(8,128)S(1)}) custom-call(f32[96,256]{1,0:T(8,128)S(1)} %collective-permute-done.2.c_in, bf16[1024,256]{1,0:T(8,128)(2,1)S(1)} %get-tuple-element.50.high_in, bf16[1024,256]{1,0:T(8,128)(2,1)S(1)} %get-tuple-element.51.low_in, s32[96,1024]{1,0:T(8,128)S(1)} %get-tuple-element.52.tile), custom_call_target="tpu_custom_call" | custom-call | flops 301989888 | bytes 1048576 | tf_op jit(solution)/shard_map/context_step/pallas_call | solution.py:208
  45.1 10.0 %all-gather = f32[384,256]{1,0:T(8,128)S(1)} all-gather(f32[96,256]{1,0:T(8,128)S(1)} %get-tuple-element.55), channel_id=2, replica_groups={{0,32,256,288},{64,96,320,352},{128,160,384,416},{192,224,448,480},{1,3..., dimensions={0}, use_global_device_ids=true | all-gather | bytes 491520 | tf_op jit(solution)/shard_map/all_gather | solution.py:292
  55.1 0.0 copy-done.2
  55.1 1.4 %pack.1 = f32[4,96,256]{2,1,0:T(8,128)} custom-call(s32[16]{0:T(128)S(1)} %copy-done.2, s32[1]{0:T(128)} %bitcast.own, f32[4,96,256]{2,1,0:T(8,128)S(1)} %bitcast.2), custom_call_target="tpu_custom_call" | custom-call | bytes 786432 | tf_op jit(solution)/shard_map/pack/pallas_call | solution.py:265
  56.5 4.8 %all-to-all-start = ((f32[4,96,256]{2,1,0:T(8,128)}), f32[4,96,256]{2,1,0:T(8,128)S(1)}, u32[]{:S(2)}, u32[]{:S(2)}) async-start(f32[4,96,256]{2,1,0:T(8,128)} %pack.1), calls=%async_computation | async-start | bytes 786432 | tf_op jit(solution)/shard_map/all_to_all | solution.py:294
  61.3 1.7 %vertex_step.8 = (f32[1024,256]{1,0:T(8,128)S(1)}, s32[96,1024]{1,0:T(8,128)S(1)}) custom-call(s32[1,1,6]{2,1,0:T(1,128)S(1)} %copy-done.1, f32[1024,256]{1,0:T(8,128)S(1)} %get-tuple-element.48.u_in, f32[96,1024]{1,0:T(8,128)S(1)} %get-tuple-element.53.r_in, f32[96,256]{1,0:T(8,128)S(1)} %collective-permute-done.2.c_in, s32[1,1,6,96,1024]{4,3,2,1,0:T(8,128)} %counts.11), custom_call_target="tpu_custom_call" | custom-call | flops 150994944 | bytes 4194304 | tf_op jit(solution)/shard_map/vertex_step/pallas_call | solution.py:235
  63.0 5.4 %all-to-all-done.received = f32[4,96,256]{2,1,0:T(8,128)S(1)} async-done(((f32[4,96,256]{2,1,0:T(8,128)}), f32[4,96,256]{2,1,0:T(8,128)S(1)}, u32[]{:S(2)}, u32[]{:S(2)}) %all-to-all-start) | async-done | bytes 393248 | tf_op jit(solution)/shard_map/all_to_all | solution.py:294
  68.4 1.5 %received_step.1 = (f32[96,256]{1,0:T(8,128)S(1)}, f32[96,1024]{1,0:T(8,128)S(1)}, f32[96,256]{1,0:T(8,128)S(1)}) custom-call(s32[16]{0:T(128)S(1)} %copy-done.2, s32[1]{0:T(128)} %bitcast.own, f32[4,96,256]{2,1,0:T(8,128)S(1)} %all-to-all-done.received, f32[1024,256]{1,0:T(8,128)S(1)} %get-tuple-element.54.u_in, s32[96,1024]{1,0:T(8,128)S(1)} %get-tuple-element.56.tile), custom_call_target="tpu_custom_call" | custom-call | flops 301989888 | bytes 1048576 | tf_op jit(solution)/shard_map/received_step/pallas_call | solution.py:220
  70.0 1.9 %collective-permute-start.3 = (f32[96,256]{1,0:T(8,128)S(1)}, f32[96,256]{1,0:T(8,128)S(1)}, u32[]{:S(2)}, u32[]{:S(2)}) collective-permute-start(f32[96,256]{1,0:T(8,128)S(1)} %get-tuple-element.60), channel_id=1, source_target_pairs={{0,1},{1,2},{2,3},{3,4},{4,5},{5,6},{6,7},{7,8},{8,9},{9,10},{10,1... | collective-permute-start | bytes 294920 | tf_op jit(solution)/shard_map/ppermute | solution.py:278
  71.9 1.7 %vertex_step.9 = (f32[1024,256]{1,0:T(8,128)S(1)}, s32[96,1024]{1,0:T(8,128)S(1)}, bf16[1024,256]{1,0:T(8,128)(2,1)S(1)}, bf16[1024,256]{1,0:T(8,128)(2,1)S(1)}) custom-call(s32[1,1,6]{2,1,0:T(1,128)S(1)} %copy-done.1, f32[1024,256]{1,0:T(8,128)S(1)} %get-tuple-element.54.u_in, f32[96,1024]{1,0:T(8,128)S(1)} %get-tuple-element.57.r_in, ...), custom_call_target="tpu_custom_call" | custom-call | flops 150994944 | bytes 4194304 | tf_op jit(solution)/shard_map/vertex_step/pallas_call | solution.py:235
  73.6 6.8 %collective-permute-done.3.c_ref = f32[96,256]{1,0:T(8,128)S(1)} collective-permute-done((f32[96,256]{1,0:T(8,128)S(1)}, f32[96,256]{1,0:T(8,128)S(1)}, u32[]{:S(2)}, u32[]{:S(2)}) %collective-permute-start.3) | collective-permute-done | bytes 98336 | tf_op jit(solution)/shard_map/ppermute | solution.py:278
  80.4 2.2 %last_step.1 = (f32[1,1,1024,256]{3,2,1,0:T(8,128)}, f32[1,1,96,256]{3,2,1,0:T(8,128)}) custom-call(f32[1024,256]{1,0:T(8,128)S(1)} %get-tuple-element.59.u_in, f32[96,256]{1,0:T(8,128)S(1)} %collective-permute-done.3.c_ref, bf16[1024,256]{1,0:T(8,128)(2,1)S(1)} %get-tuple-element.61.high_in, bf16[1024,256]{1,0:T(8,128)(2,1)S(1)} %get-tuple-element.62.low_in, ...), custom_call_target="tpu_custom_call" | custom-call | flops 452984832 | bytes 2097152 | tf_op jit(solution)/shard_map/last_step/pallas_call | solution.py:248
Async XLA Ops:
  0.6 0.7 copy-start
  4.6 16.8 %collective-permute-start = (f32[96,256]{1,0:T(8,128)S(1)}, f32[96,256]{1,0:T(8,128)S(1)}, u32[]{:S(2)}, u32[]{:S(2)}) collective-permute-start(f32[96,256]{1,0:T(8,128)S(1)} %get-tuple-element.37), channel_id=1, source_target_pairs={{0,1},{1,2},{2,3},{3,4},{4,5},{5,6},{6,7},{7,8},{8,9},{9,10},{10,1... | collective-permute-start | bytes 294920 | tf_op jit(solution)/shard_map/ppermute | solution.py:278
  22.3 10.4 %collective-permute-start.1 = (f32[96,256]{1,0:T(8,128)S(1)}, f32[96,256]{1,0:T(8,128)S(1)}, u32[]{:S(2)}, u32[]{:S(2)}) collective-permute-start(f32[96,256]{1,0:T(8,128)S(1)} %get-tuple-element.43), channel_id=1, source_target_pairs={{0,1},{1,2},{2,3},{3,4},{4,5},{5,6},{6,7},{7,8},{8,9},{9,10},{10,1... | collective-permute-start | bytes 294920 | tf_op jit(solution)/shard_map/ppermute | solution.py:278
  24.3 11.4 %copy-start.1 = (s32[1,1,6]{2,1,0:T(1,128)S(1)}, s32[1,1,6]{2,1,0:T(1,128)}, u32[]{:S(2)}) copy-start(s32[1,1,6]{2,1,0:T(1,128)} %order.11) | copy-start | bytes 76
  33.7 10.4 %collective-permute-start.2 = (f32[96,256]{1,0:T(8,128)S(1)}, f32[96,256]{1,0:T(8,128)S(1)}, u32[]{:S(2)}, u32[]{:S(2)}) collective-permute-start(f32[96,256]{1,0:T(8,128)S(1)} %get-tuple-element.49), channel_id=1, source_target_pairs={{0,1},{1,2},{2,3},{3,4},{4,5},{5,6},{6,7},{7,8},{8,9},{9,10},{10,1... | collective-permute-start | bytes 294920 | tf_op jit(solution)/shard_map/ppermute | solution.py:278
  35.7 19.5 %copy-start.2 = (s32[16]{0:T(128)S(1)}, s32[16]{0:T(128)}, u32[]{:S(2)}) copy-start(s32[16]{0:T(128)} %matching.3) | copy-start | bytes 196
  56.5 11.9 %all-to-all-start = ((f32[4,96,256]{2,1,0:T(8,128)}), f32[4,96,256]{2,1,0:T(8,128)S(1)}, u32[]{:S(2)}, u32[]{:S(2)}) async-start(f32[4,96,256]{2,1,0:T(8,128)} %pack.1), calls=%async_computation | async-start | bytes 786432 | tf_op jit(solution)/shard_map/all_to_all | solution.py:294
  70.0 10.4 %collective-permute-start.3 = (f32[96,256]{1,0:T(8,128)S(1)}, f32[96,256]{1,0:T(8,128)S(1)}, u32[]{:S(2)}, u32[]{:S(2)}) collective-permute-start(f32[96,256]{1,0:T(8,128)S(1)} %get-tuple-element.60), channel_id=1, source_target_pairs={{0,1},{1,2},{2,3},{3,4},{4,5},{5,6},{6,7},{7,8},{8,9},{9,10},{10,1... | collective-permute-start | bytes 294920 | tf_op jit(solution)/shard_map/ppermute | solution.py:278

commit v2 on v1

--- a/solution.py
+++ b/solution.py
@@ -26,14 +26,14 @@
     return jax.ShapeDtypeStruct(shape, dtype)
 
 
-def call(kernel, name, out_shape, in_specs, out_specs, flops, moved, scratch=()):
+def call(kernel, out_shape, in_specs, out_specs, flops, moved, scratch=(), aliases=None):
     return pl.pallas_call(
         kernel,
         out_shape=out_shape,
         in_specs=in_specs,
         out_specs=out_specs,
         scratch_shapes=scratch,
-        name=name,
+        input_output_aliases=aliases or {},
         cost_estimate=pl.CostEstimate(flops=flops, bytes_accessed=moved, transcendentals=CR * VR),
         compiler_params=pltpu.CompilerParams(vmem_limit_bytes=16 * 1024 * 1024),
     )
@@ -96,8 +96,7 @@
     c_out[...] = c - lr_rate * total
 
 
-def context_kernel(c_in, high_in, low_in, tile, c_out, r_out):
-    c = c_in[...]
+def context_update(c, high_in, low_in, tile, c_out, r_out):
     ch, cl = halves(c)
     cc = jnp.concatenate([ch, cl], 0)
     total = jnp.zeros((CR, D), F32)
@@ -108,6 +107,36 @@
         r_out[:, rows] = r
         total = total + context_part(*halves(r), high, low)
     c_out[...] = c - lr_rate * total
+
+
+def is_odd():
+    return lax.rem(lax.axis_index("blk"), 2) == 1
+
+
+def odd_kernel(moved, high_in, low_in, tile, c_out, r_out, c_in, passed):
+    del passed
+
+    @pl.when(is_odd())
+    def _():
+        c = moved[...]
+        c_in[...] = c
+        context_update(c, high_in, low_in, tile, c_out, r_out)
+
+
+def even_kernel(moved, high_in, low_in, tile, passed, r_old, c_old, c_out, r_out, c_in):
+    del passed, r_old, c_old
+
+    @pl.when(jnp.logical_not(is_odd()))
+    def _():
+        c = moved[...]
+        c_in[...] = c
+        context_update(c, high_in, low_in, tile, c_out, r_out)
+
+
+def both_kernel(from_even, from_odd, high_in, low_in, tile, c_out, r_out, c_in):
+    c = jnp.where(is_odd(), from_even[...], from_odd[...])
+    c_in[...] = c
+    context_update(c, high_in, low_in, tile, c_out, r_out)
 
 
 def source_group(matching, group):
@@ -129,7 +158,7 @@
         out[x] = held[(source // (N_X * N_CORE)) * N_CORE + source % N_CORE]
 
 
-def received_kernel(matching, own, received, u_in, tile, c_out, r_out, c_in):
+def received_update(matching, own, received, u_in, tile, c_out, r_out, c_in):
     c = received[x_of(source_group(matching, own[0]))]
     c_in[...] = c
     ch, cl = halves(c)
@@ -142,6 +171,27 @@
         r_out[:, rows] = r
         total = total + context_part(*halves(r), high, low)
     c_out[...] = c - lr_rate * total
+
+
+def odd_received_kernel(*refs):
+    *refs, passed = refs
+    del passed
+
+    @pl.when(is_odd())
+    def _():
+        received_update(*refs)
+
+
+def even_received_kernel(matching, own, received, u_in, tile, passed, r_old, c_old, *outs):
+    del passed, r_old, c_old
+
+    @pl.when(jnp.logical_not(is_odd()))
+    def _():
+        received_update(matching, own, received, u_in, tile, *outs)
+
+
+def gate_kernel(passed, out):
+    del passed, out
 
 
 def vertex_kernel(order, u_in, r_in, c_in, counts, u_out, tile, *rest, step):
@@ -159,8 +209,8 @@
     copy.wait()
 
 
-def last_kernel(u_in, c_ref, high_in, low_in, tile, vertex_out, context_out, u_new, c_new, sems):
-    c = c_ref[...]
+def last_kernel(u_in, from_even, from_odd, high_in, low_in, tile, vertex_out, context_out, u_new, c_new, sems):
+    c = jnp.where(is_odd(), from_even[...], from_odd[...])
     ch, cl = halves(c)
     cc = jnp.concatenate([ch, cl], 0)
     double = jnp.concatenate([ch, ch], 0)
@@ -185,7 +235,6 @@
 
 MATMUL = 6 * CR * VR * D
 BLOCK = 4 * CR * D
-GRADIENT = 4 * CR * VR
 VERTEX = 4 * VR * D
 
 UPDATED = (array((CR, D)), array((CR, VR)), array((CR, D)))
@@ -194,7 +243,6 @@
 def first_step(order, vertex, context, counts):
     return call(
         first_kernel,
-        "first_step",
         UPDATED + (array((VR, D)),),
         [SMEM, HBM, HBM, HBM],
         (VMEM,) * 4,
@@ -204,28 +252,52 @@
     )(order, vertex, context, counts)
 
 
-def context_step(c, high, low, tile):
-    return call(
-        context_kernel,
-        "context_step",
-        UPDATED[:2],
-        [VMEM] * 4,
-        (VMEM,) * 2,
+PASSED = array((8, 128))
+
+
+def gate(passed):
+    return call(gate_kernel, PASSED, [VMEM], VMEM, 0, 8 * 128 * 4)(passed)
+
+
+def odd_step(moved, high, low, tile):
+    return call(
+        odd_kernel, UPDATED + (PASSED,), [VMEM] * 4, (VMEM,) * 4, 2 * MATMUL, VERTEX
+    )(moved, high, low, tile)
+
+
+def even_step(moved, high, low, tile, passed, r, c):
+    return call(
+        even_kernel, UPDATED, [VMEM] * 7, (VMEM,) * 3, 2 * MATMUL, VERTEX, aliases={5: 1, 6: 2}
+    )(moved, high, low, tile, passed, r, c)
+
+
+def both_step(from_even, from_odd, high, low, tile):
+    return call(
+        both_kernel, UPDATED, [VMEM] * 5, (VMEM,) * 3, 2 * MATMUL, VERTEX
+    )(from_even, from_odd, high, low, tile)
+
+
+def odd_received_step(matching, own, received, u, tile):
+    return call(
+        odd_received_kernel,
+        UPDATED + (PASSED,),
+        [SMEM] * 2 + [VMEM] * 3,
+        (VMEM,) * 4,
         2 * MATMUL,
         VERTEX,
-    )(c, high, low, tile)
-
-
-def received_step(matching, own, received, u, tile):
-    return call(
-        received_kernel,
-        "received_step",
+    )(matching, own, received, u, tile)
+
+
+def even_received_step(matching, own, received, u, tile, passed, r, c):
+    return call(
+        even_received_kernel,
         UPDATED,
-        [SMEM] * 2 + [VMEM] * 3,
+        [SMEM] * 2 + [VMEM] * 6,
         (VMEM,) * 3,
         2 * MATMUL,
         VERTEX,
-    )(matching, own, received, u, tile)
+        aliases={6: 1, 7: 2},
+    )(matching, own, received, u, tile, passed, r, c)
 
 
 def vertex_step(order, u, r, c, counts, step):
@@ -234,7 +306,6 @@
         outs += (array((VR, D), BF16),) * 2
     return call(
         functools.partial(vertex_kernel, step=step),
-        "vertex_step",
         outs,
         [SMEM, VMEM, VMEM, VMEM, HBM],
         (VMEM,) * len(outs),
@@ -244,12 +315,11 @@
     )(order, u, r, c, counts)
 
 
-def last_step(u, c, high, low, tile):
+def last_step(u, from_even, from_odd, high, low, tile):
     return call(
         last_kernel,
-        "last_step",
         (array((1, 1, VR, D)), array((1, 1, CR, D))),
-        [VMEM] * 5,
+        [VMEM] * 6,
         (HBM, HBM),
         3 * MATMUL,
         2 * VERTEX,
@@ -258,24 +328,18 @@
             pltpu.VMEM((CR, D), F32),
             pltpu.SemaphoreType.DMA((PARTS + 1,)),
         ],
-    )(u, c, high, low, tile)
+    )(u, from_even, from_odd, high, low, tile)
 
 
 def pack(matching, own, held):
     return call(
-        pack_kernel,
-        "pack",
-        array((N_X, CR, D)),
-        [SMEM, SMEM, VMEM],
-        VMEM,
-        0,
-        8 * BLOCK,
+        pack_kernel, array((N_X, CR, D)), [SMEM, SMEM, VMEM], VMEM, 0, 8 * BLOCK
     )(matching, own, held)
 
 
-def shifted(block):
+def shifted(block, parity):
     devices = lax.axis_size("blk")
-    return lax.ppermute(block, "blk", [(i, (i + 1) % devices) for i in range(devices)])
+    return lax.ppermute(block, "blk", [(i, (i + 1) % devices) for i in range(parity, devices, 2)])
 
 
 def on_device(vertex, context, counts, tile_index, matching):
@@ -286,22 +350,30 @@
     half = N_X * N_CORE
     columns = [[g, g + 1, g + half, g + half + 1] for g in range(0, half, N_CORE)]
     rings = [[y * half + x * N_CORE + k for x in range(N_X)] for y in range(2) for k in range(N_CORE)]
-    c_new, r, c, u = first_step(tile_index, vertex, context, counts)
+    c_odd, r, c, u = first_step(tile_index, vertex, context, counts)
+    c_even = c_odd
     for step in range(1, STEPS):
         if step == FIRST:
-            held = lax.all_gather(c_new, "grp", axis_index_groups=columns)
+            held = lax.all_gather(c_odd, "grp", axis_index_groups=columns)
             sent = pack(matching, own, held)
             moved = lax.all_to_all(sent, "grp", 0, 0, axis_index_groups=rings, tiled=True)
         else:
-            moved = shifted(c_new)
+            from_odd = shifted(c_odd, 1)
+            from_even = shifted(c_even, 0)
         u, tile, *split = vertex_step(tile_index, u, r, c, counts, step)
         if step == STEPS - 1:
-            return last_step(u, moved, *split, tile)
+            return last_step(u, from_even, from_odd, *split, tile)
+        if step == FIRST - 1:
+            c_odd, r, c = both_step(from_even, from_odd, *split, tile)
+            continue
         if step == FIRST:
-            c_new, r, c = received_step(matching, own, moved, u, tile)
+            seen = (matching, own, moved, u, tile)
+            odd, even, seen_even = odd_received_step, even_received_step, seen
         else:
-            c = moved
-            c_new, r = context_step(c, *split, tile)
+            odd, even, seen, seen_even = odd_step, even_step, (from_even, *split, tile), (from_odd, *split, tile)
+        c_odd, r, c, passed = odd(*seen)
+        passed = gate(passed)
+        c_even, r, c = even(*seen_even, passed, r, c)
 
 
 def solution(mesh):

time: 83.1 us -> 88.3 us (1.063)
  starting transfers between devices: 14.1 us -> 17.4 us
  waiting for transfers between devices: 37.3 us -> 38.4 us
    ppermute x4 -> x8, starting transfers between devices: 9.25 us -> 12.5 us  [shifted(): lax.ppermute(block, 'blk', [(i, (i + 1) % devices) for i in range(parity,...]
    ppermute x4 -> x8, waiting for transfers between devices: 31.9 us -> 33 us  [shifted(): lax.ppermute(block, 'blk', [(i, (i + 1) % devices) for i in range(parity,...]
    pallas_call x12 -> x18, Pallas kernels: 19.7 us -> 20.4 us  [the longest x5 8.53 us: vertex_step(): call(functools.partial(vertex_kernel, step=step), outs, [SMEM, VMEM, VMEM...]
  transfers between devices with their start and end apart: 5 -> 9, of which waited for: 5 -> 5; matrix products, arithmetic and copies ran while one was open for 0% -> 0% of each run, Pallas kernels for 10% -> 10%
where the time goes in v2:
time: 88.3 us; the launch traced here: 87.7 us
  waiting for transfers between devices  38.4 us (43%)
  Pallas kernels  20.4 us (23%)
  starting transfers between devices  17.4 us (20%)
  blocking collectives  10 us (11%)
  between operations  0.89 us (1%)
    ppermute x8, waiting for transfers between devices, shifted(): lax.ppermute(block, 'blk', [(i, (i + 1) % devices) for i in range(parity,...  33 us
    ppermute x8, starting transfers between devices, shifted(): lax.ppermute(block, 'blk', [(i, (i + 1) % devices) for i in range(parity,...  12.5 us
    all_gather x1, blocking collectives, on_device(): held = lax.all_gather(c_odd, 'grp', axis_index_groups=columns)  10 us
    pallas_call x5, Pallas kernels, vertex_step(): call(functools.partial(vertex_kernel, step=step), outs, [SMEM, VMEM, VMEM...  8.53 us
    all_to_all x1, waiting for transfers between devices, on_device(): lax.all_to_all(sent, 'grp', 0, 0, axis_index_groups=rings, tiled=True)  5.41 us
    all_to_all x1, starting transfers between devices, on_device(): lax.all_to_all(sent, 'grp', 0, 0, axis_index_groups=rings, tiled=True)  4.82 us
    pallas_call x1, Pallas kernels, first_step(): call(first_kernel, UPDATED + (array((VR, D)),), [SMEM, HBM, HBM, HBM], (V...  3.31 us
    pallas_call x1, Pallas kernels, last_step(): call(last_kernel, (array((1, 1, VR, D)), array((1, 1, CR, D))), [VMEM] *...  2.2 us
  transfers between devices with their start and end apart: 9, of which 5 were waited for; matrix products, arithmetic and copies ran while one was open for 0% of the time, Pallas kernels for 10%

profile of v2, /device:TPU:2, one launch (start us, length us, event | category | flops | bytes accessed | tf_op | source)
XLA Modules:
  0.0 87.7 jit_solution(9684724388880224392)
XLA Ops:
  0.6 0.0 copy-start
  0.6 0.6 copy-done
  1.3 3.3 %shard_map.68 = (f32[96,256]{1,0:T(8,128)S(1)}, f32[96,1024]{1,0:T(8,128)S(1)}, f32[96,256]{1,0:T(8,128)S(1)}, f32[1024,256]{1,0:T(8,128)S(1)}) custom-call(s32[1,1,6]{2,1,0:T(1,128)S(1)} %copy-done, f32[1,1,1024,256]{3,2,1,0:T(8,128)} %vertex.1, f32[1,1,96,256]{3,2,1,0:T(8,128)} %context.1, s32[1,1,6,96,1024]{4,3,2,1,0:T(8,128)} %counts.11), custom_call_target="tpu_custom_call" | custom-call | flops 301989888 | bytes 2097152 | tf_op jit(solution)/shard_map/pallas_call | solution.py:244
  4.6 3.5 %collective-permute-start.1 = (f32[96,256]{1,0:T(8,128)S(1)}, f32[96,256]{1,0:T(8,128)S(1)}, u32[]{:S(2)}, u32[]{:S(2)}) collective-permute-start(f32[96,256]{1,0:T(8,128)S(1)} %get-tuple-element.52), channel_id=1, source_target_pairs={{0,1},{2,3},{4,5},{6,7},{8,9},{10,11},{12,13},{14,15},{16,17},{18,... | collective-permute-start | bytes 294920 | tf_op jit(solution)/shard_map/ppermute | solution.py:342
  8.1 1.3 %collective-permute-start = (f32[96,256]{1,0:T(8,128)S(1)}, f32[96,256]{1,0:T(8,128)S(1)}, u32[]{:S(2)}, u32[]{:S(2)}) collective-permute-start(f32[96,256]{1,0:T(8,128)S(1)} %get-tuple-element.52), channel_id=1, source_target_pairs={{1,2},{3,4},{5,6},{7,8},{9,10},{11,12},{13,14},{15,16},{17,18},{19... | collective-permute-start | bytes 294920 | tf_op jit(solution)/shard_map/ppermute | solution.py:342
  9.4 1.7 %shard_map.69 = (f32[1024,256]{1,0:T(8,128)S(1)}, s32[96,1024]{1,0:T(8,128)S(1)}, bf16[1024,256]{1,0:T(8,128)(2,1)S(1)}, bf16[1024,256]{1,0:T(8,128)(2,1)S(1)}) custom-call(s32[1,1,6]{2,1,0:T(1,128)S(1)} %copy-done, f32[1024,256]{1,0:T(8,128)S(1)} %get-tuple-element.48.u_in, f32[96,1024]{1,0:T(8,128)S(1)} %get-tuple-element.49.r_in, ...), custom_call_target="tpu_custom_call" | custom-call | flops 150994944 | bytes 4194304 | tf_op jit(solution)/shard_map/pallas_call | solution.py:307
  11.1 0.0 copy-start.1
  11.2 10.9 %collective-permute-done.moved = f32[96,256]{1,0:T(8,128)S(1)} collective-permute-done((f32[96,256]{1,0:T(8,128)S(1)}, f32[96,256]{1,0:T(8,128)S(1)}, u32[]{:S(2)}, u32[]{:S(2)}) %collective-permute-start) | collective-permute-done | bytes 98336 | tf_op jit(solution)/shard_map/ppermute | solution.py:342
  22.0 1.0 %shard_map.72 = (f32[96,256]{1,0:T(8,128)S(1)}, f32[96,1024]{1,0:T(8,128)S(1)}, f32[96,256]{1,0:T(8,128)S(1)}) custom-call(f32[96,256]{1,0:T(8,128)S(1)} %collective-permute-done.moved, bf16[1024,256]{1,0:T(8,128)(2,1)S(1)} %get-tuple-element.53.high_in, ...), custom_call_target="tpu_custom_call", output_to_operand_aliasing={{1}: (5, {}), {2}: (6, {})} | custom-call | flops 301989888 | bytes 1048576 | tf_op jit(solution)/shard_map/pallas_call | solution.py:269
  23.0 1.3 %collective-permute-start.3 = (f32[96,256]{1,0:T(8,128)S(1)}, f32[96,256]{1,0:T(8,128)S(1)}, u32[]{:S(2)}, u32[]{:S(2)}) collective-permute-start(f32[96,256]{1,0:T(8,128)S(1)} %get-tuple-element.66), channel_id=1, source_target_pairs={{0,1},{2,3},{4,5},{6,7},{8,9},{10,11},{12,13},{14,15},{16,17},{18,... | collective-permute-start | bytes 294920 | tf_op jit(solution)/shard_map/ppermute | solution.py:342
  24.3 1.3 %collective-permute-start.2 = (f32[96,256]{1,0:T(8,128)S(1)}, f32[96,256]{1,0:T(8,128)S(1)}, u32[]{:S(2)}, u32[]{:S(2)}) collective-permute-start(f32[96,256]{1,0:T(8,128)S(1)} %get-tuple-element.62), channel_id=1, source_target_pairs={{1,2},{3,4},{5,6},{7,8},{9,10},{11,12},{13,14},{15,16},{17,18},{19... | collective-permute-start | bytes 294920 | tf_op jit(solution)/shard_map/ppermute | solution.py:342
  25.6 1.7 %shard_map.73 = (f32[1024,256]{1,0:T(8,128)S(1)}, s32[96,1024]{1,0:T(8,128)S(1)}, bf16[1024,256]{1,0:T(8,128)(2,1)S(1)}, bf16[1024,256]{1,0:T(8,128)(2,1)S(1)}) custom-call(s32[1,1,6]{2,1,0:T(1,128)S(1)} %copy-done.1, f32[1024,256]{1,0:T(8,128)S(1)} %get-tuple-element.51.u_in, f32[96,1024]{1,0:T(8,128)S(1)} %get-tuple-element.59.r_in, ...), custom_call_target="tpu_custom_call" | custom-call | flops 150994944 | bytes 4194304 | tf_op jit(solution)/shard_map/pallas_call | solution.py:307
  27.4 7.3 %collective-permute-done.2.moved = f32[96,256]{1,0:T(8,128)S(1)} collective-permute-done((f32[96,256]{1,0:T(8,128)S(1)}, f32[96,256]{1,0:T(8,128)S(1)}, u32[]{:S(2)}, u32[]{:S(2)}) %collective-permute-start.2) | collective-permute-done | bytes 98336 | tf_op jit(solution)/shard_map/ppermute | solution.py:342
  34.7 1.0 %shard_map.76 = (f32[96,256]{1,0:T(8,128)S(1)}, f32[96,1024]{1,0:T(8,128)S(1)}, f32[96,256]{1,0:T(8,128)S(1)}) custom-call(f32[96,256]{1,0:T(8,128)S(1)} %collective-permute-done.2.moved, bf16[1024,256]{1,0:T(8,128)(2,1)S(1)} %get-tuple-element.63.high_in, ...), custom_call_target="tpu_custom_call", output_to_operand_aliasing={{1}: (5, {}), {2}: (6, {})} | custom-call | flops 301989888 | bytes 1048576 | tf_op jit(solution)/shard_map/pallas_call | solution.py:269
  35.7 1.3 %collective-permute-start.4 = (f32[96,256]{1,0:T(8,128)S(1)}, f32[96,256]{1,0:T(8,128)S(1)}, u32[]{:S(2)}, u32[]{:S(2)}) collective-permute-start(f32[96,256]{1,0:T(8,128)S(1)} %get-tuple-element.73), channel_id=1, source_target_pairs={{0,1},{2,3},{4,5},{6,7},{8,9},{10,11},{12,13},{14,15},{16,17},{18,... | collective-permute-start | bytes 294920 | tf_op jit(solution)/shard_map/ppermute | solution.py:342
  37.0 1.3 %collective-permute-start.5 = (f32[96,256]{1,0:T(8,128)S(1)}, f32[96,256]{1,0:T(8,128)S(1)}, u32[]{:S(2)}, u32[]{:S(2)}) collective-permute-start(f32[96,256]{1,0:T(8,128)S(1)} %get-tuple-element.74), channel_id=1, source_target_pairs={{1,2},{3,4},{5,6},{7,8},{9,10},{11,12},{13,14},{15,16},{17,18},{19... | collective-permute-start | bytes 294920 | tf_op jit(solution)/shard_map/ppermute | solution.py:342
  38.3 0.0 copy-start.2
  38.3 1.7 %shard_map.77 = (f32[1024,256]{1,0:T(8,128)S(1)}, s32[96,1024]{1,0:T(8,128)S(1)}, bf16[1024,256]{1,0:T(8,128)(2,1)S(1)}, bf16[1024,256]{1,0:T(8,128)(2,1)S(1)}) custom-call(s32[1,1,6]{2,1,0:T(1,128)S(1)} %copy-done.1, f32[1024,256]{1,0:T(8,128)S(1)} %get-tuple-element.61.u_in, f32[96,1024]{1,0:T(8,128)S(1)} %get-tuple-element.70.r_in, ...), custom_call_target="tpu_custom_call" | custom-call | flops 150994944 | bytes 4194304 | tf_op jit(solution)/shard_map/pallas_call | solution.py:307
  40.0 7.4 %collective-permute-done.5.from_odd = f32[96,256]{1,0:T(8,128)S(1)} collective-permute-done((f32[96,256]{1,0:T(8,128)S(1)}, f32[96,256]{1,0:T(8,128)S(1)}, u32[]{:S(2)}, u32[]{:S(2)}) %collective-permute-start.5) | collective-permute-done | bytes 98336 | tf_op jit(solution)/shard_map/ppermute | solution.py:342
  47.4 0.9 %shard_map.78 = (f32[96,256]{1,0:T(8,128)S(1)}, f32[96,1024]{1,0:T(8,128)S(1)}, f32[96,256]{1,0:T(8,128)S(1)}) custom-call(f32[96,256]{1,0:T(8,128)S(1)} %collective-permute-done.4.from_even, f32[96,256]{1,0:T(8,128)S(1)} %collective-permute-done.5.from_odd, bf16[1024,256]{1,0:T(8,128)(2,1)S(1)} %get-tuple-element.75.high_in, ...), custom_call_target="tpu_custom_call" | custom-call | flops 301989888 | bytes 1048576 | tf_op jit(solution)/shard_map/pallas_call | solution.py:275
  48.4 10.0 %all-gather = f32[384,256]{1,0:T(8,128)S(1)} all-gather(f32[96,256]{1,0:T(8,128)S(1)} %get-tuple-element.81), channel_id=2, replica_groups={{0,32,256,288},{64,96,320,352},{128,160,384,416},{192,224,448,480},{1,3..., dimensions={0}, use_global_device_ids=true | all-gather | bytes 491520 | tf_op jit(solution)/shard_map/all_gather | solution.py:357
  58.4 1.4 %shard_map.80 = f32[4,96,256]{2,1,0:T(8,128)} custom-call(s32[16]{0:T(128)S(1)} %copy-done.2, s32[1]{0:T(128)} %bitcast.own.refs_1_, f32[4,96,256]{2,1,0:T(8,128)S(1)} %bitcast.2), custom_call_target="tpu_custom_call" | custom-call | bytes 786432 | tf_op jit(solution)/shard_map/pallas_call | solution.py:335
  59.8 4.8 %all-to-all-start = ((f32[4,96,256]{2,1,0:T(8,128)}), f32[4,96,256]{2,1,0:T(8,128)S(1)}, u32[]{:S(2)}, u32[]{:S(2)}) async-start(f32[4,96,256]{2,1,0:T(8,128)} %shard_map.80), calls=%async_computation | async-start | bytes 786432 | tf_op jit(solution)/shard_map/all_to_all | solution.py:359
  64.6 1.7 %shard_map.79 = (f32[1024,256]{1,0:T(8,128)S(1)}, s32[96,1024]{1,0:T(8,128)S(1)}) custom-call(s32[1,1,6]{2,1,0:T(1,128)S(1)} %copy-done.1, f32[1024,256]{1,0:T(8,128)S(1)} %get-tuple-element.72.u_in, f32[96,1024]{1,0:T(8,128)S(1)} %get-tuple-element.78.r_in, f32[96,256]{1,0:T(8,128)S(1)} %get-tuple-element.79.c_in, s32[1,1,6,96,1024]{4,3,2,1,0:T(8,128)} %counts.11), custom_call_target="tpu_custom_call" | custom-call | flops 150994944 | bytes 4194304 | tf_op jit(solution)/shard_map/pallas_call | solution.py:307
  66.3 5.4 %all-to-all-done.refs_2_.received = f32[4,96,256]{2,1,0:T(8,128)S(1)} async-done(((f32[4,96,256]{2,1,0:T(8,128)}), f32[4,96,256]{2,1,0:T(8,128)S(1)}, u32[]{:S(2)}, u32[]{:S(2)}) %all-to-all-start) | async-done | bytes 393248 | tf_op jit(solution)/shard_map/all_to_all | solution.py:359
  71.7 0.6 shard_map.81
  72.3 1.5 %shard_map.83 = (f32[96,256]{1,0:T(8,128)S(1)}, f32[96,1024]{1,0:T(8,128)S(1)}, f32[96,256]{1,0:T(8,128)S(1)}) custom-call(s32[16]{0:T(128)S(1)} %copy-done.2, s32[1]{0:T(128)} %bitcast.own.refs_1_, f32[4,96,256]{2,1,0:T(8,128)S(1)} %all-to-all-done.refs_2_.received, ...), custom_call_target="tpu_custom_call", output_to_operand_aliasing={{1}: (6, {}), {2}: (7, {})} | custom-call | flops 301989888 | bytes 1048576 | tf_op jit(solution)/shard_map/pallas_call | solution.py:292
  73.8 1.3 %collective-permute-start.6 = (f32[96,256]{1,0:T(8,128)S(1)}, f32[96,256]{1,0:T(8,128)S(1)}, u32[]{:S(2)}, u32[]{:S(2)}) collective-permute-start(f32[96,256]{1,0:T(8,128)S(1)} %get-tuple-element.89), channel_id=1, source_target_pairs={{0,1},{2,3},{4,5},{6,7},{8,9},{10,11},{12,13},{14,15},{16,17},{18,... | collective-permute-start | bytes 294920 | tf_op jit(solution)/shard_map/ppermute | solution.py:342
  75.1 1.3 %collective-permute-start.7 = (f32[96,256]{1,0:T(8,128)S(1)}, f32[96,256]{1,0:T(8,128)S(1)}, u32[]{:S(2)}, u32[]{:S(2)}) collective-permute-start(f32[96,256]{1,0:T(8,128)S(1)} %get-tuple-element.90), channel_id=1, source_target_pairs={{1,2},{3,4},{5,6},{7,8},{9,10},{11,12},{13,14},{15,16},{17,18},{19... | collective-permute-start | bytes 294920 | tf_op jit(solution)/shard_map/ppermute | solution.py:342
  76.4 1.7 %shard_map.84 = (f32[1024,256]{1,0:T(8,128)S(1)}, s32[96,1024]{1,0:T(8,128)S(1)}, bf16[1024,256]{1,0:T(8,128)(2,1)S(1)}, bf16[1024,256]{1,0:T(8,128)(2,1)S(1)}) custom-call(s32[1,1,6]{2,1,0:T(1,128)S(1)} %copy-done.1, f32[1024,256]{1,0:T(8,128)S(1)} %get-tuple-element.80.refs_3_.u_in, f32[96,1024]{1,0:T(8,128)S(1)} %get-tuple-element.86.r_in, ...), custom_call_target="tpu_custom_call" | custom-call | flops 150994944 | bytes 4194304 | tf_op jit(solution)/shard_map/pallas_call | solution.py:307
  78.2 7.4 %collective-permute-done.7.from_odd = f32[96,256]{1,0:T(8,128)S(1)} collective-permute-done((f32[96,256]{1,0:T(8,128)S(1)}, f32[96,256]{1,0:T(8,128)S(1)}, u32[]{:S(2)}, u32[]{:S(2)}) %collective-permute-start.7) | collective-permute-done | bytes 98336 | tf_op jit(solution)/shard_map/ppermute | solution.py:342
  85.6 2.2 %shard_map.85 = (f32[1,1,1024,256]{3,2,1,0:T(8,128)}, f32[1,1,96,256]{3,2,1,0:T(8,128)}) custom-call(f32[1024,256]{1,0:T(8,128)S(1)} %get-tuple-element.88.u_in, f32[96,256]{1,0:T(8,128)S(1)} %collective-permute-done.6.from_even, f32[96,256]{1,0:T(8,128)S(1)} %collective-permute-done.7.from_odd, bf16[1024,256]{1,0:T(8,128)(2,1)S(1)} %get-tuple-element.91.high_in, ...), custom_call_target="tpu_custom_call" | custom-call | flops 452984832 | bytes 2097152 | tf_op jit(solution)/shard_map/pallas_call | solution.py:319
  (11 shorter events, 0.1 us)
Async XLA Ops:
  0.6 0.7 copy-start
  4.6 6.5 %collective-permute-start.1 = (f32[96,256]{1,0:T(8,128)S(1)}, f32[96,256]{1,0:T(8,128)S(1)}, u32[]{:S(2)}, u32[]{:S(2)}) collective-permute-start(f32[96,256]{1,0:T(8,128)S(1)} %get-tuple-element.52), channel_id=1, source_target_pairs={{0,1},{2,3},{4,5},{6,7},{8,9},{10,11},{12,13},{14,15},{16,17},{18,... | collective-permute-start | bytes 294920 | tf_op jit(solution)/shard_map/ppermute | solution.py:342
  8.1 14.0 %collective-permute-start = (f32[96,256]{1,0:T(8,128)S(1)}, f32[96,256]{1,0:T(8,128)S(1)}, u32[]{:S(2)}, u32[]{:S(2)}) collective-permute-start(f32[96,256]{1,0:T(8,128)S(1)} %get-tuple-element.52), channel_id=1, source_target_pairs={{1,2},{3,4},{5,6},{7,8},{9,10},{11,12},{13,14},{15,16},{17,18},{19... | collective-permute-start | bytes 294920 | tf_op jit(solution)/shard_map/ppermute | solution.py:342
  11.1 14.5 %copy-start.1 = (s32[1,1,6]{2,1,0:T(1,128)S(1)}, s32[1,1,6]{2,1,0:T(1,128)}, u32[]{:S(2)}) copy-start(s32[1,1,6]{2,1,0:T(1,128)} %order.11) | copy-start | bytes 76
  23.0 4.3 %collective-permute-start.3 = (f32[96,256]{1,0:T(8,128)S(1)}, f32[96,256]{1,0:T(8,128)S(1)}, u32[]{:S(2)}, u32[]{:S(2)}) collective-permute-start(f32[96,256]{1,0:T(8,128)S(1)} %get-tuple-element.66), channel_id=1, source_target_pairs={{0,1},{2,3},{4,5},{6,7},{8,9},{10,11},{12,13},{14,15},{16,17},{18,... | collective-permute-start | bytes 294920 | tf_op jit(solution)/shard_map/ppermute | solution.py:342
  24.3 10.4 %collective-permute-start.2 = (f32[96,256]{1,0:T(8,128)S(1)}, f32[96,256]{1,0:T(8,128)S(1)}, u32[]{:S(2)}, u32[]{:S(2)}) collective-permute-start(f32[96,256]{1,0:T(8,128)S(1)} %get-tuple-element.62), channel_id=1, source_target_pairs={{1,2},{3,4},{5,6},{7,8},{9,10},{11,12},{13,14},{15,16},{17,18},{19... | collective-permute-start | bytes 294920 | tf_op jit(solution)/shard_map/ppermute | solution.py:342
  35.7 4.3 %collective-permute-start.4 = (f32[96,256]{1,0:T(8,128)S(1)}, f32[96,256]{1,0:T(8,128)S(1)}, u32[]{:S(2)}, u32[]{:S(2)}) collective-permute-start(f32[96,256]{1,0:T(8,128)S(1)} %get-tuple-element.73), channel_id=1, source_target_pairs={{0,1},{2,3},{4,5},{6,7},{8,9},{10,11},{12,13},{14,15},{16,17},{18,... | collective-permute-start | bytes 294920 | tf_op jit(solution)/shard_map/ppermute | solution.py:342
  37.0 10.4 %collective-permute-start.5 = (f32[96,256]{1,0:T(8,128)S(1)}, f32[96,256]{1,0:T(8,128)S(1)}, u32[]{:S(2)}, u32[]{:S(2)}) collective-permute-start(f32[96,256]{1,0:T(8,128)S(1)} %get-tuple-element.74), channel_id=1, source_target_pairs={{1,2},{3,4},{5,6},{7,8},{9,10},{11,12},{13,14},{15,16},{17,18},{19... | collective-permute-start | bytes 294920 | tf_op jit(solution)/shard_map/ppermute | solution.py:342
  38.3 20.1 %copy-start.2 = (s32[16]{0:T(128)S(1)}, s32[16]{0:T(128)}, u32[]{:S(2)}) copy-start(s32[16]{0:T(128)} %matching.3) | copy-start | bytes 196
  59.8 11.9 %all-to-all-start = ((f32[4,96,256]{2,1,0:T(8,128)}), f32[4,96,256]{2,1,0:T(8,128)S(1)}, u32[]{:S(2)}, u32[]{:S(2)}) async-start(f32[4,96,256]{2,1,0:T(8,128)} %shard_map.80), calls=%async_computation | async-start | bytes 786432 | tf_op jit(solution)/shard_map/all_to_all | solution.py:359
  73.8 4.3 %collective-permute-start.6 = (f32[96,256]{1,0:T(8,128)S(1)}, f32[96,256]{1,0:T(8,128)S(1)}, u32[]{:S(2)}, u32[]{:S(2)}) collective-permute-start(f32[96,256]{1,0:T(8,128)S(1)} %get-tuple-element.89), channel_id=1, source_target_pairs={{0,1},{2,3},{4,5},{6,7},{8,9},{10,11},{12,13},{14,15},{16,17},{18,... | collective-permute-start | bytes 294920 | tf_op jit(solution)/shard_map/ppermute | solution.py:342
  75.1 10.4 %collective-permute-start.7 = (f32[96,256]{1,0:T(8,128)S(1)}, f32[96,256]{1,0:T(8,128)S(1)}, u32[]{:S(2)}, u32[]{:S(2)}) collective-permute-start(f32[96,256]{1,0:T(8,128)S(1)} %get-tuple-element.90), channel_id=1, source_target_pairs={{1,2},{3,4},{5,6},{7,8},{9,10},{11,12},{13,14},{15,16},{17,18},{19... | collective-permute-start | bytes 294920 | tf_op jit(solution)/shard_map/ppermute | solution.py:342

commit v3 on v1

v3 whole, which is shorter than its diff:
```python
import functools

import jax
import jax.numpy as jnp
from jax import lax
from jax.experimental import pallas as pl
from jax.experimental.pallas import tpu as pltpu
from jax.sharding import PartitionSpec as P

STEPS = 6
FIRST = 4
CR, VR, D = 96, 1024, 256
N_X, N_CORE = 4, 2
N_GRP = 16
lr_rate = 0.003

F32, BF16 = jnp.float32, jnp.bfloat16
CHUNK = 256
PARTS = VR // CHUNK
VMEM = pl.BlockSpec(memory_space=pltpu.VMEM)
SMEM = pl.BlockSpec(memory_space=pltpu.SMEM)
HBM = pl.BlockSpec(memory_space=pltpu.HBM)


def array(shape, dtype=F32):
    return jax.ShapeDtypeStruct(shape, dtype)


def call(kernel, out_shape, in_specs, out_specs, flops, moved, scratch=(), aliases=None):
    return pl.pallas_call(
        kernel,
        out_shape=out_shape,
        in_specs=in_specs,
        out_specs=out_specs,
        scratch_shapes=scratch,
        input_output_aliases=aliases or {},
        cost_estimate=pl.CostEstimate(flops=flops, bytes_accessed=moved, transcendentals=CR * VR),
        compiler_params=pltpu.CompilerParams(vmem_limit_bytes=16 * 1024 * 1024),
    )


def halves(x):
    high = x.astype(BF16)
    return high, (x - high.astype(F32)).astype(BF16)


def product(a, b, a_dim, b_dim):
    return lax.dot_general(a, b, (((a_dim,), (b_dim,)), ((), ())), preferred_element_type=F32)


def logits_of(ch, cc, high, low):
    both = product(cc, high, 1, 1)
    return both[:CR] + (both[CR:] + product(ch, low, 1, 1))


def gradient_of(logits, weight):
    weight = weight.astype(F32)
    return (weight + 1.0) * jax.nn.sigmoid(logits) - weight


def logit_gradient(ch, cc, high, low, weight):
    return gradient_of(logits_of(ch, cc, high, low), weight)


def context_part(rh, rl, high, low):
    both = product(jnp.concatenate([rh, rl], 0), high, 1, 0)
    return both[:CR] + (both[CR:] + product(rh, low, 1, 0))


def vertex_part(rh, rl, double, cl):
    return product(jnp.concatenate([rh, rl], 0), double, 0, 0) + product(rh, cl, 0, 0)


def rows_of(part):
    return pl.ds(part * CHUNK, CHUNK)


def first_kernel(
    order_hbm, vertex, context, counts, c_out, r_out, c_in, u_out, order, tile, highs, lows, sems
):
    order_copy = pltpu.make_async_copy(order_hbm.at[0, 0], order, sems.at[0])
    order_copy.start()
    c_copy = pltpu.make_async_copy(context.at[0, 0], c_in, sems.at[1])
    c_copy.start()
    u_copies = []
    for part in range(PARTS):
        rows = rows_of(part)
        u_copies.append(
            pltpu.make_async_copy(vertex.at[0, 0, rows, :], u_out.at[rows, :], sems.at[3 + part])
        )
        u_copies[-1].start()
    order_copy.wait()
    tile_copy = pltpu.make_async_copy(counts.at[0, 0, order[0]], tile, sems.at[2])
    tile_copy.start()
    c_copy.wait()
    c = c_in[...]
    ch, cl = halves(c)
    cc = jnp.concatenate([ch, cl], 0)
    for part in range(PARTS):
        rows = rows_of(part)
        u_copies[part].wait()
        high, low = halves(u_out[rows, :])
        highs[rows, :], lows[rows, :] = high, low
        r_out[:, rows] = logits_of(ch, cc, high, low)
    tile_copy.wait()
    total = jnp.zeros((CR, D), F32)
    for part in range(PARTS):
        rows = rows_of(part)
        r = gradient_of(r_out[:, rows], tile[:, rows])
        r_out[:, rows] = r
        total = total + context_part(*halves(r), highs[rows, :], lows[rows, :])
    c_out[...] = c - lr_rate * total


def context_update(c, high_in, low_in, tile, c_out, r_out):
    ch, cl = halves(c)
    cc = jnp.concatenate([ch, cl], 0)
    total = jnp.zeros((CR, D), F32)
    for part in range(PARTS):
        rows = rows_of(part)
        high, low = high_in[rows, :], low_in[rows, :]
        r = logit_gradient(ch, cc, high, low, tile[:, rows])
        r_out[:, rows] = r
        total = total + context_part(*halves(r), high, low)
    c_out[...] = c - lr_rate * total


def member(places):
    place = lax.rem(lax.axis_index("blk"), N_PLACES)
    return functools.reduce(jnp.logical_or, [place == p for p in places])


def take(blocks, targets, c_in):
    for block, places in zip(blocks, targets):

        @pl.when(member(places))
        def _(block=block):
            c_in[...] = block[...]


def context_kernel(*refs, places, targets, first):
    blocks, refs = refs[: len(targets)], refs[len(targets) :]
    high_in, low_in, tile = refs[:3]
    c_out, r_out, c_in = refs[3 if first else 5 :][:3]

    @pl.when(member(places))
    def _():
        take(blocks, targets, c_in)
        context_update(c_in[...], high_in, low_in, tile, c_out, r_out)


def source_group(matching, group):
    source = jnp.int32(0)
    for k in range(N_GRP):
        source = jnp.where(matching[k] == group, jnp.int32(k), source)
    return source


def x_of(group):
    return lax.rem(group // N_CORE, N_X)


def pack_kernel(matching, held, out, chosen, sems):
    group = lax.axis_index("grp")
    base = group - x_of(group) * N_CORE
    copies = []
    for x in range(N_X):
        source = source_group(matching, base + x * N_CORE)
        slot = (source // (N_X * N_CORE)) * N_CORE + lax.rem(source, N_CORE)
        copies.append(pltpu.make_async_copy(held.at[slot], out.at[x], sems.at[x]))
        copies[-1].start()
    chosen[...] = jnp.full(chosen.shape, x_of(source_group(matching, group)), jnp.int32)
    for copy in copies:
        copy.wait()


def received_kernel(*refs, places, first):
    chosen, received, u_in, tile = refs[:4]
    c_out, r_out, c_in = refs[4 if first else 7 :][:3]

    @pl.when(member(places))
    def _():
        from_x = chosen[0:1, 0:1]
        c = received[0]
        for x in range(1, N_X):
            c = jnp.where(from_x == x, received[x], c)
        c_in[...] = c
        ch, cl = halves(c)
        cc = jnp.concatenate([ch, cl], 0)
        total = jnp.zeros((CR, D), F32)
        for part in range(PARTS):
            rows = rows_of(part)
            high, low = halves(u_in[rows, :])
            r = logit_gradient(ch, cc, high, low, tile[:, rows])
            r_out[:, rows] = r
            total = total + context_part(*halves(r), high, low)
        c_out[...] = c - lr_rate * total


def gate_kernel(passed, out):
    del passed, out


def vertex_kernel(*refs, step, places, skipped, split):
    order, u_in, r_in, c_in, counts = refs[:5]
    u_out, tile, *halves_out, sem = refs[5 + skipped :]
    del split

    @pl.when(member(places))
    def _():
        lane = lax.broadcasted_iota(jnp.int32, (1, STEPS), 1)
        stored = jnp.max(jnp.where(lane == step, order[0], 0))
        copy = pltpu.make_async_copy(counts.at[0, 0, stored], tile, sem)
        copy.start()
        ch, cl = halves(c_in[...])
        double = jnp.concatenate([ch, ch], 0)
        for part in range(PARTS):
            rows = rows_of(part)
            u = u_in[rows, :] - lr_rate * vertex_part(*halves(r_in[:, rows]), double, cl)
            u_out[rows, :] = u
            for half_out, half in zip(halves_out, halves(u)):
                half_out[rows, :] = half
        copy.wait()


def last_kernel(*refs, targets):
    blocks, refs = refs[: len(targets)], refs[len(targets) :]
    u_in, high_in, low_in, tile, vertex_out, context_out, u_new, c_new, sems = refs
    take(blocks, targets, c_new)
    c = c_new[...]
    ch, cl = halves(c)
    cc = jnp.concatenate([ch, cl], 0)
    double = jnp.concatenate([ch, ch], 0)
    total = jnp.zeros((CR, D), F32)
    copies = []
    for part in range(PARTS):
        rows = rows_of(part)
        high, low = high_in[rows, :], low_in[rows, :]
        rh, rl = halves(logit_gradient(ch, cc, high, low, tile[:, rows]))
        u_new[rows, :] = u_in[rows, :] - lr_rate * vertex_part(rh, rl, double, cl)
        copies.append(
            pltpu.make_async_copy(u_new.at[rows, :], vertex_out.at[0, 0, rows, :], sems.at[part])
        )
        copies[-1].start()
        total = total + context_part(rh, rl, high, low)
    c_new[...] = c - lr_rate * total
    copies.append(pltpu.make_async_copy(c_new, context_out.at[0, 0], sems.at[PARTS]))
    copies[-1].start()
    for copy in copies:
        copy.wait()


MATMUL = 6 * CR * VR * D
BLOCK = 4 * CR * D
VERTEX = 4 * VR * D

UPDATED = (array((CR, D)), array((CR, VR)), array((CR, D)))


def first_step(order, vertex, context, counts):
    return call(
        first_kernel,
        UPDATED + (array((VR, D)),),
        [HBM] * 4,
        (VMEM,) * 4,
        2 * MATMUL,
        2 * VERTEX,
        [
            pltpu.SMEM((STEPS,), jnp.int32),
            pltpu.VMEM((CR, VR), jnp.int32),
            pltpu.VMEM((VR, D), BF16),
            pltpu.VMEM((VR, D), BF16),
            pltpu.SemaphoreType.DMA((3 + PARTS,)),
        ],
    )(order, vertex, context, counts)


PASSED = array((8, 128))


def gate(passed):
    return call(gate_kernel, PASSED, [VMEM], VMEM, 0, 8 * 128 * 4)(passed)


def context_step(places, blocks, targets, state, kept, last):
    first = not kept
    inputs = (*blocks, *state, *kept)
    at = len(blocks) + len(state)
    outs = UPDATED + (PASSED,) * (not last)
    return call(
        functools.partial(context_kernel, places=places, targets=targets, first=first),
        outs,
        [VMEM] * len(inputs),
        (VMEM,) * len(outs),
        2 * MATMUL,
        VERTEX,
        aliases=None if first else {at: 1, at + 1: 2},
    )(*inputs)


def received_step(places, chosen, received, u, tile, passed, kept, last):
    first = not kept
    inputs = (chosen, received, u, tile)
    if not first:
        inputs += (passed, *kept)
    outs = UPDATED + (PASSED,) * (not last)
    return call(
        functools.partial(received_kernel, places=places, first=first),
        outs,
        [VMEM] * len(inputs),
        (VMEM,) * len(outs),
        2 * MATMUL,
        VERTEX,
        aliases=None if first else {5: 1, 6: 2},
    )(*inputs)


def vertex_step(places, order, u, r, c, counts, step, passed, kept):
    split = step != FIRST
    outs = (array((VR, D)), array((CR, VR), jnp.int32)) + (array((VR, D), BF16),) * (2 * split)
    skipped = () if passed is None else (passed, *kept)
    aliases = {1: 0}
    if passed is not None:
        aliases.update({6 + k: 1 + k for k in range(len(kept))})
    return call(
        functools.partial(
            vertex_kernel, step=step, places=places, skipped=len(skipped), split=split
        ),
        outs,
        [VMEM, VMEM, VMEM, VMEM, HBM] + [VMEM] * len(skipped),
        (VMEM,) * len(outs),
        MATMUL,
        4 * VERTEX,
        [pltpu.SemaphoreType.DMA],
        aliases=aliases,
    )(order, u, r, c, counts, *skipped)


def last_step(u, high, low, tile, blocks, targets):
    return call(
        functools.partial(last_kernel, targets=targets),
        (array((1, 1, VR, D)), array((1, 1, CR, D))),
        [VMEM] * (4 + len(blocks)),
        (HBM, HBM),
        3 * MATMUL,
        2 * VERTEX,
        [
            pltpu.VMEM((VR, D), F32),
            pltpu.VMEM((CR, D), F32),
            pltpu.SemaphoreType.DMA((PARTS + 1,)),
        ],
    )(*blocks, u, high, low, tile)


def pack(matching, held):
    return call(
        pack_kernel,
        (array((N_X, CR, D)), array((8, 128), jnp.int32)),
        [SMEM, VMEM],
        (HBM, VMEM),
        0,
        8 * BLOCK,
        [pltpu.SemaphoreType.DMA((N_X,))],
    )(matching, held)


N_PLACES = 4
EVERY = (0, 1, 2, 3)
ORDER = {
    0: ((1, 2), (0, 3)),
    1: ((2,), (3,), (0, 1)),
    2: ((3,), (0, 1, 2)),
    3: (EVERY,),
    4: ((1, 2, 3), (0,)),
}


def shifted(block, places):
    devices = lax.axis_size("blk")
    route = [(i, (i + 1) % devices) for i in range(devices) if i % N_PLACES in places]
    return lax.ppermute(block, "blk", route)


def after(places):
    return {(p + 1) % N_PLACES for p in places}


def sources(places, step):
    served = [(k, sorted(after(group) & set(places))) for k, group in enumerate(ORDER[step - 1])]
    return [(k, tuple(group)) for k, group in served if group]


def on_device(vertex, context, counts, tile_index, matching):
    order = pltpu.with_memory_space_constraint(tile_index, pltpu.HBM)
    vertex, context, counts = (
        pltpu.with_memory_space_constraint(x, pltpu.HBM) for x in (vertex, context, counts)
    )
    half = N_X * N_CORE
    columns = [[g, g + 1, g + half, g + half + 1] for g in range(0, half, N_CORE)]
    rings = [[y * half + x * N_CORE + k for x in range(N_X)] for y in range(2) for k in range(N_CORE)]

    def send(block, step, k):
        return shifted(block, ORDER[step][k])

    c_new, r, c, u = first_step(order, vertex, context, counts)
    moved = [send(c_new, 0, k) for k in range(len(ORDER[0]))]
    for step in range(1, STEPS - 1):
        if step == FIRST:
            held = lax.all_gather(c_new, "grp", axis_index_groups=columns)
            sent, chosen = pack(matching, held)
            received = lax.all_to_all(sent, "grp", 0, 0, axis_index_groups=rings, tiled=True)
            u, tile = vertex_step(EVERY, tile_index, u, r, c, counts, step, None, ())
        new, passed, state, kept = [], None, (), ()
        for k, places in enumerate(ORDER[step]):
            if step != FIRST:
                u, *state = vertex_step(
                    places, tile_index, u, r, c, counts, step, passed, tuple(state)
                )
            last = k + 1 == len(ORDER[step])
            if step == FIRST:
                c_new, *kept = received_step(places, chosen, received, u, tile, passed, kept, last)
            else:
                tile, high, low = state
                wanted = sources(places, step)
                c_new, *kept = context_step(
                    places,
                    [moved[j] for j, _ in wanted],
                    [group for _, group in wanted],
                    (high, low, tile),
                    kept,
                    last,
                )
            if not last:
                *kept, passed = kept
            if step != FIRST - 1:
                new.append(send(c_new, step, k))
            if k + 1 < len(ORDER[step]):
                passed = gate(passed)
        moved = new
        r, c = kept
    step = STEPS - 1
    u, tile, high, low = vertex_step(EVERY, tile_index, u, r, c, counts, step, None, ())
    wanted = sources(EVERY, step)
    return last_step(u, high, low, tile, [moved[j] for j, _ in wanted], [g for _, g in wanted])


def solution(mesh):
    in_specs = (
        P("grp", "blk", None, None),
        P("grp", "blk", None, None),
        P("grp", "blk", None, None, None),
        P("grp", "blk", None),
        P(),
    )
    out_specs = (P("grp", "blk", None, None), P("grp", "blk", None, None))
    return jax.shard_map(
        on_device, mesh=mesh, in_specs=in_specs, out_specs=out_specs, check_vma=False
    )
```

time: 83.1 us -> 86 us (1.035)
  starting transfers between devices: 14.1 us -> 20.2 us
  Pallas kernels: 19.7 us -> 17.7 us
    ppermute x4 -> x9, starting transfers between devices: 9.25 us -> 15.4 us  [shifted(): return lax.ppermute(block, 'blk', route)]
    pallas_call x12 -> x23, Pallas kernels: 19.7 us -> 17.7 us  [the longest x8 7.64 us: vertex_step(): call(functools.partial(vertex_kernel, step=step, places=places, skipped=l...]
    ppermute x4 -> x9, waiting for transfers between devices: 31.9 us -> 30.8 us  [shifted(): return lax.ppermute(block, 'blk', route)]
  transfers between devices with their start and end apart: 5 -> 10, of which waited for: 5 -> 6; matrix products, arithmetic and copies ran while one was open for 0% -> 0% of each run, Pallas kernels for 10% -> 10%
where the time goes in v3:
time: 86 us; the launch traced here: 85.5 us
  waiting for transfers between devices  36.5 us (42%)
  starting transfers between devices  20.2 us (23%)
  Pallas kernels  17.7 us (21%)
  blocking collectives  10 us (12%)
  between operations  0.92 us (1%)
    ppermute x9, waiting for transfers between devices, shifted(): return lax.ppermute(block, 'blk', route)  30.8 us
    ppermute x9, starting transfers between devices, shifted(): return lax.ppermute(block, 'blk', route)  15.4 us
    all_gather x1, blocking collectives, on_device(): held = lax.all_gather(c_new, 'grp', axis_index_groups=columns)  10 us
    pallas_call x8, Pallas kernels, vertex_step(): call(functools.partial(vertex_kernel, step=step, places=places, skipped=l...  7.64 us
    all_to_all x1, waiting for transfers between devices, on_device(): lax.all_to_all(sent, 'grp', 0, 0, axis_index_groups=rings, tiled=True)  5.65 us
    all_to_all x1, starting transfers between devices, on_device(): lax.all_to_all(sent, 'grp', 0, 0, axis_index_groups=rings, tiled=True)  4.84 us
    pallas_call x6, Pallas kernels, context_step(): call(functools.partial(context_kernel, places=places, targets=targets, fi...  2.92 us
    pallas_call x1, Pallas kernels, first_step(): call(first_kernel, UPDATED + (array((VR, D)),), [HBM] * 4, (VMEM,) * 4, 2...  2.66 us
  transfers between devices with their start and end apart: 10, of which 6 were waited for; matrix products, arithmetic and copies ran while one was open for 0% of the time, Pallas kernels for 10%

profile of v3, /device:TPU:2, one launch (start us, length us, event | category | flops | bytes accessed | tf_op | source)
XLA Modules:
  0.0 85.5 jit_solution(12867266512272194124)
XLA Ops:
  0.6 2.7 %shard_map.68 = (f32[96,256]{1,0:T(8,128)S(1)}, f32[96,1024]{1,0:T(8,128)S(1)}, f32[96,256]{1,0:T(8,128)S(1)}, f32[1024,256]{1,0:T(8,128)S(1)}) custom-call(s32[1,1,6]{2,1,0:T(1,128)} %refs_0_.15, f32[1,1,1024,256]{3,2,1,0:T(8,128)} %vertex.1, f32[1,1,96,256]{3,2,1,0:T(8,128)} %context.1, s32[1,1,6,96,1024]{4,3,2,1,0:T(8,128)} %refs_4_.15), custom_call_target="tpu_custom_call" | custom-call | flops 301989888 | bytes 2097152 | tf_op jit(solution)/shard_map/pallas_call | solution.py:261
  3.3 0.7 collective-permute-start
  4.0 6.3 %collective-permute-start.2 = (f32[96,256]{1,0:T(8,128)S(1)}, f32[96,256]{1,0:T(8,128)S(1)}, u32[]{:S(2)}, u32[]{:S(2)}) collective-permute-start(f32[96,256]{1,0:T(8,128)S(1)} %get-tuple-element.66), channel_id=1, source_target_pairs={{0,1},{3,4},{4,5},{7,8},{8,9},{11,12},{12,13},{15,16},{16,17},{19,... | collective-permute-start | bytes 294920 | tf_op jit(solution)/shard_map/ppermute | solution.py:381
  10.3 0.0 collective-permute-done.refs_0_
  10.5 0.7 collective-permute-start.1
  11.1 1.5 %shard_map.75 = (f32[1024,256]{1,0:T(8,128)S(1)}, s32[96,1024]{1,0:T(8,128)S(1)}, bf16[1024,256]{1,0:T(8,128)(2,1)S(1)}, bf16[1024,256]{1,0:T(8,128)(2,1)S(1)}) custom-call(s32[1,1,6]{2,1,0:T(1,128)S(1)} %copy-done, f32[1024,256]{1,0:T(8,128)S(1)} %get-tuple-element.76.refs_1_, ...), custom_call_target="tpu_custom_call", output_to_operand_aliasing={{0}: (1, {}), {1}: (6, {}), {2}: (7, {}), {3}: (8, {})} | custom-call | flops 150994944 | bytes 4194304 | tf_op jit(solution)/shard_map/pallas_call | solution.py:325
  12.7 8.1 %collective-permute-done.2.refs_0_ = f32[96,256]{1,0:T(8,128)S(1)} collective-permute-done((f32[96,256]{1,0:T(8,128)S(1)}, f32[96,256]{1,0:T(8,128)S(1)}, u32[]{:S(2)}, u32[]{:S(2)}) %collective-permute-start.2) | collective-permute-done | bytes 98336 | tf_op jit(solution)/shard_map/ppermute | solution.py:381
  20.8 1.0 %shard_map.76 = (f32[96,256]{1,0:T(8,128)S(1)}, f32[96,1024]{1,0:T(8,128)S(1)}, f32[96,256]{1,0:T(8,128)S(1)}) custom-call(f32[96,256]{1,0:T(8,128)S(1)} %collective-permute-done.2.refs_0_, bf16[1024,256]{1,0:T(8,128)(2,1)S(1)} %get-tuple-element.84.refs_1_, ...), custom_call_target="tpu_custom_call", output_to_operand_aliasing={{1}: (4, {}), {2}: (5, {})} | custom-call | flops 301989888 | bytes 1048576 | tf_op jit(solution)/shard_map/pallas_call | solution.py:290
  21.7 1.3 %collective-permute-start.5 = (f32[96,256]{1,0:T(8,128)S(1)}, f32[96,256]{1,0:T(8,128)S(1)}, u32[]{:S(2)}, u32[]{:S(2)}) collective-permute-start(f32[96,256]{1,0:T(8,128)S(1)} %get-tuple-element.96), channel_id=1, source_target_pairs={{0,1},{1,2},{4,5},{5,6},{8,9},{9,10},{12,13},{13,14},{16,17},{17,1... | collective-permute-start | bytes 294920 | tf_op jit(solution)/shard_map/ppermute | solution.py:381
  23.0 1.3 %collective-permute-start.4 = (f32[96,256]{1,0:T(8,128)S(1)}, f32[96,256]{1,0:T(8,128)S(1)}, u32[]{:S(2)}, u32[]{:S(2)}) collective-permute-start(f32[96,256]{1,0:T(8,128)S(1)} %get-tuple-element.95), channel_id=1, source_target_pairs={{3,4},{7,8},{11,12},{15,16},{19,20},{23,24},{27,28},{31,0},{35,36}... | collective-permute-start | bytes 294920 | tf_op jit(solution)/shard_map/ppermute | solution.py:381
  24.4 0.0 collective-permute-done.1.refs_0_
  24.4 1.5 %shard_map.80 = (f32[1024,256]{1,0:T(8,128)S(1)}, s32[96,1024]{1,0:T(8,128)S(1)}, bf16[1024,256]{1,0:T(8,128)(2,1)S(1)}, bf16[1024,256]{1,0:T(8,128)(2,1)S(1)}) custom-call(s32[1,1,6]{2,1,0:T(1,128)S(1)} %copy-done, f32[1024,256]{1,0:T(8,128)S(1)} %get-tuple-element.97.refs_1_, ...), custom_call_target="tpu_custom_call", output_to_operand_aliasing={{0}: (1, {}), {1}: (6, {}), {2}: (7, {}), {3}: (8, {})} | custom-call | flops 150994944 | bytes 4194304 | tf_op jit(solution)/shard_map/pallas_call | solution.py:325
  25.9 7.5 %collective-permute-done.4.refs_0_ = f32[96,256]{1,0:T(8,128)S(1)} collective-permute-done((f32[96,256]{1,0:T(8,128)S(1)}, f32[96,256]{1,0:T(8,128)S(1)}, u32[]{:S(2)}, u32[]{:S(2)}) %collective-permute-start.4) | collective-permute-done | bytes 98336 | tf_op jit(solution)/shard_map/ppermute | solution.py:381
  33.4 1.0 %shard_map.81 = (f32[96,256]{1,0:T(8,128)S(1)}, f32[96,1024]{1,0:T(8,128)S(1)}, f32[96,256]{1,0:T(8,128)S(1)}) custom-call(f32[96,256]{1,0:T(8,128)S(1)} %collective-permute-done.4.refs_0_, f32[96,256]{1,0:T(8,128)S(1)} %collective-permute-done.5.refs_1_, ...), custom_call_target="tpu_custom_call", output_to_operand_aliasing={{1}: (5, {}), {2}: (6, {})} | custom-call | flops 301989888 | bytes 1048576 | tf_op jit(solution)/shard_map/pallas_call | solution.py:290
  34.4 1.3 %collective-permute-start.6 = (f32[96,256]{1,0:T(8,128)S(1)}, f32[96,256]{1,0:T(8,128)S(1)}, u32[]{:S(2)}, u32[]{:S(2)}) collective-permute-start(f32[96,256]{1,0:T(8,128)S(1)} %get-tuple-element.104), channel_id=1, source_target_pairs={{0,1},{1,2},{2,3},{4,5},{5,6},{6,7},{8,9},{9,10},{10,11},{12,13},{... | collective-permute-start | bytes 294920 | tf_op jit(solution)/shard_map/ppermute | solution.py:381
  35.7 1.3 %collective-permute-start.3 = (f32[96,256]{1,0:T(8,128)S(1)}, f32[96,256]{1,0:T(8,128)S(1)}, u32[]{:S(2)}, u32[]{:S(2)}) collective-permute-start(f32[96,256]{1,0:T(8,128)S(1)} %get-tuple-element.94), channel_id=1, source_target_pairs={{3,4},{7,8},{11,12},{15,16},{19,20},{23,24},{27,28},{31,0},{35,36}... | collective-permute-start | bytes 294920 | tf_op jit(solution)/shard_map/ppermute | solution.py:381
  37.0 0.0 copy-start.1
  37.0 1.5 %shard_map.82 = (f32[1024,256]{1,0:T(8,128)S(1)}, s32[96,1024]{1,0:T(8,128)S(1)}, bf16[1024,256]{1,0:T(8,128)(2,1)S(1)}, bf16[1024,256]{1,0:T(8,128)(2,1)S(1)}) custom-call(s32[1,1,6]{2,1,0:T(1,128)S(1)} %copy-done, f32[1024,256]{1,0:T(8,128)S(1)} %get-tuple-element.105.refs_1_, ...), custom_call_target="tpu_custom_call", output_to_operand_aliasing={{0}: (1, {})} | custom-call | flops 150994944 | bytes 4194304 | tf_op jit(solution)/shard_map/pallas_call | solution.py:325
  38.5 0.4 collective-permute-done.6.refs_1_
  38.9 7.3 %collective-permute-done.3.refs_0_ = f32[96,256]{1,0:T(8,128)S(1)} collective-permute-done((f32[96,256]{1,0:T(8,128)S(1)}, f32[96,256]{1,0:T(8,128)S(1)}, u32[]{:S(2)}, u32[]{:S(2)}) %collective-permute-start.3) | collective-permute-done | bytes 98336 | tf_op jit(solution)/shard_map/ppermute | solution.py:381
  46.2 1.0 %shard_map.83 = (f32[96,256]{1,0:T(8,128)S(1)}, f32[96,1024]{1,0:T(8,128)S(1)}, f32[96,256]{1,0:T(8,128)S(1)}) custom-call(f32[96,256]{1,0:T(8,128)S(1)} %collective-permute-done.3.refs_0_, f32[96,256]{1,0:T(8,128)S(1)} %collective-permute-done.6.refs_1_, bf16[1024,256]{1,0:T(8,128)(2,1)S(1)} %get-tuple-element.108.refs_2_, ...), custom_call_target="tpu_custom_call" | custom-call | flops 301989888 | bytes 1048576 | tf_op jit(solution)/shard_map/pallas_call | solution.py:290
  47.2 10.0 %all-gather = f32[384,256]{1,0:T(8,128)S(1)} all-gather(f32[96,256]{1,0:T(8,128)S(1)} %get-tuple-element.111), channel_id=2, replica_groups={{0,32,256,288},{64,96,320,352},{128,160,384,416},{192,224,448,480},{1,3..., dimensions={0}, use_global_device_ids=true | all-gather | bytes 491520 | tf_op jit(solution)/shard_map/all_gather | solution.py:409
  57.2 1.3 %shard_map.84 = (f32[4,96,256]{2,1,0:T(8,128)}, s32[8,128]{1,0:T(8,128)S(1)}) custom-call(s32[16]{0:T(128)S(1)} %copy-done.1, f32[4,96,256]{2,1,0:T(8,128)S(1)} %bitcast.1), custom_call_target="tpu_custom_call" | custom-call | bytes 786432 | tf_op jit(solution)/shard_map/pallas_call | solution.py:356
  58.6 4.8 %all-to-all-start = ((f32[4,96,256]{2,1,0:T(8,128)}), f32[4,96,256]{2,1,0:T(8,128)S(1)}, u32[]{:S(2)}, u32[]{:S(2)}) async-start(f32[4,96,256]{2,1,0:T(8,128)} %get-tuple-element.113), calls=%async_computation | async-start | bytes 786432 | tf_op jit(solution)/shard_map/all_to_all | solution.py:411
  63.4 1.5 %shard_map.85 = (f32[1024,256]{1,0:T(8,128)S(1)}, s32[96,1024]{1,0:T(8,128)S(1)}) custom-call(s32[1,1,6]{2,1,0:T(1,128)S(1)} %copy-done, f32[1024,256]{1,0:T(8,128)S(1)} %get-tuple-element.114.refs_1_, f32[96,1024]{1,0:T(8,128)S(1)} %get-tuple-element.115.refs_2_, f32[96,256]{1,0:T(8,128)S(1)} %get-tuple-element.116.refs_3_, ...), custom_call_target="tpu_custom_call", output_to_operand_aliasing={{0}: (1, {})} | custom-call | flops 150994944 | bytes 4194304 | tf_op jit(solution)/shard_map/pallas_call | solution.py:325
  64.9 5.6 %all-to-all-done.refs_1_ = f32[4,96,256]{2,1,0:T(8,128)S(1)} async-done(((f32[4,96,256]{2,1,0:T(8,128)}), f32[4,96,256]{2,1,0:T(8,128)S(1)}, u32[]{:S(2)}, u32[]{:S(2)}) %all-to-all-start) | async-done | bytes 393248 | tf_op jit(solution)/shard_map/all_to_all | solution.py:411
  70.6 1.0 %shard_map.88 = (f32[96,256]{1,0:T(8,128)S(1)}, f32[96,1024]{1,0:T(8,128)S(1)}, f32[96,256]{1,0:T(8,128)S(1)}) custom-call(s32[8,128]{1,0:T(8,128)S(1)} %get-tuple-element.112.refs_0_, f32[4,96,256]{2,1,0:T(8,128)S(1)} %all-to-all-done.refs_1_, f32[1024,256]{1,0:T(8,128)S(1)} %get-tuple-element.117.refs_2_.refs_1_, ...), custom_call_target="tpu_custom_call", output_to_operand_aliasing={{1}: (5, {}), {2}: (6, {})} | custom-call | flops 301989888 | bytes 1048576 | tf_op jit(solution)/shard_map/pallas_call | solution.py:307
  71.5 1.3 %collective-permute-start.8 = (f32[96,256]{1,0:T(8,128)S(1)}, f32[96,256]{1,0:T(8,128)S(1)}, u32[]{:S(2)}, u32[]{:S(2)}) collective-permute-start(f32[96,256]{1,0:T(8,128)S(1)} %get-tuple-element.123), channel_id=1, source_target_pairs={{0,1},{4,5},{8,9},{12,13},{16,17},{20,21},{24,25},{28,29},{32,33},... | collective-permute-start | bytes 294920 | tf_op jit(solution)/shard_map/ppermute | solution.py:381
  72.8 1.3 %collective-permute-start.7 = (f32[96,256]{1,0:T(8,128)S(1)}, f32[96,256]{1,0:T(8,128)S(1)}, u32[]{:S(2)}, u32[]{:S(2)}) collective-permute-start(f32[96,256]{1,0:T(8,128)S(1)} %get-tuple-element.119), channel_id=1, source_target_pairs={{1,2},{2,3},{3,4},{5,6},{6,7},{7,8},{9,10},{10,11},{11,12},{13,14}... | collective-permute-start | bytes 294920 | tf_op jit(solution)/shard_map/ppermute | solution.py:381
  74.1 1.5 %shard_map.89 = (f32[1024,256]{1,0:T(8,128)S(1)}, s32[96,1024]{1,0:T(8,128)S(1)}, bf16[1024,256]{1,0:T(8,128)(2,1)S(1)}, bf16[1024,256]{1,0:T(8,128)(2,1)S(1)}) custom-call(s32[1,1,6]{2,1,0:T(1,128)S(1)} %copy-done, f32[1024,256]{1,0:T(8,128)S(1)} %get-tuple-element.117.refs_2_.refs_1_, ...), custom_call_target="tpu_custom_call", output_to_operand_aliasing={{0}: (1, {})} | custom-call | flops 150994944 | bytes 4194304 | tf_op jit(solution)/shard_map/pallas_call | solution.py:325
  75.7 7.6 %collective-permute-done.7.refs_0_ = f32[96,256]{1,0:T(8,128)S(1)} collective-permute-done((f32[96,256]{1,0:T(8,128)S(1)}, f32[96,256]{1,0:T(8,128)S(1)}, u32[]{:S(2)}, u32[]{:S(2)}) %collective-permute-start.7) | collective-permute-done | bytes 98336 | tf_op jit(solution)/shard_map/ppermute | solution.py:381
  83.3 2.2 %shard_map.90 = (f32[1,1,1024,256]{3,2,1,0:T(8,128)}, f32[1,1,96,256]{3,2,1,0:T(8,128)}) custom-call(f32[96,256]{1,0:T(8,128)S(1)} %collective-permute-done.7.refs_0_, f32[96,256]{1,0:T(8,128)S(1)} %collective-permute-done.8.refs_1_, f32[1024,256]{1,0:T(8,128)S(1)} %get-tuple-element.126.refs_2_, bf16[1024,256]{1,0:T(8,128)(2,1)S(1)} %get-tuple-element.127.refs_3_, ...), custom_call_target="tpu_custom_call" | custom-call | flops 452984832 | bytes 2097152 | tf_op jit(solution)/shard_map/pallas_call | solution.py:340
  (16 shorter events, 0.1 us)
Async XLA Ops:
  0.6 9.7 %copy-start = (s32[1,1,6]{2,1,0:T(1,128)S(1)}, s32[1,1,6]{2,1,0:T(1,128)}, u32[]{:S(2)}) copy-start(s32[1,1,6]{2,1,0:T(1,128)} %refs_0_.15) | copy-start | bytes 76
  3.3 7.0 %collective-permute-start = (f32[96,256]{1,0:T(8,128)S(1)}, f32[96,256]{1,0:T(8,128)S(1)}, u32[]{:S(2)}, u32[]{:S(2)}) collective-permute-start(f32[96,256]{1,0:T(8,128)S(1)} %get-tuple-element.66), channel_id=1, source_target_pairs={{1,2},{2,3},{5,6},{6,7},{9,10},{10,11},{13,14},{14,15},{17,18},{18... | collective-permute-start | bytes 294920 | tf_op jit(solution)/shard_map/ppermute | solution.py:381
  4.0 16.8 %collective-permute-start.2 = (f32[96,256]{1,0:T(8,128)S(1)}, f32[96,256]{1,0:T(8,128)S(1)}, u32[]{:S(2)}, u32[]{:S(2)}) collective-permute-start(f32[96,256]{1,0:T(8,128)S(1)} %get-tuple-element.66), channel_id=1, source_target_pairs={{0,1},{3,4},{4,5},{7,8},{8,9},{11,12},{12,13},{15,16},{16,17},{19,... | collective-permute-start | bytes 294920 | tf_op jit(solution)/shard_map/ppermute | solution.py:381
  10.5 13.9 %collective-permute-start.1 = (f32[96,256]{1,0:T(8,128)S(1)}, f32[96,256]{1,0:T(8,128)S(1)}, u32[]{:S(2)}, u32[]{:S(2)}) collective-permute-start(f32[96,256]{1,0:T(8,128)S(1)} %get-tuple-element.73), channel_id=1, source_target_pairs={{2,3},{6,7},{10,11},{14,15},{18,19},{22,23},{26,27},{30,31},{34,35... | collective-permute-start | bytes 294920 | tf_op jit(solution)/shard_map/ppermute | solution.py:381
  21.7 4.2 %collective-permute-start.5 = (f32[96,256]{1,0:T(8,128)S(1)}, f32[96,256]{1,0:T(8,128)S(1)}, u32[]{:S(2)}, u32[]{:S(2)}) collective-permute-start(f32[96,256]{1,0:T(8,128)S(1)} %get-tuple-element.96), channel_id=1, source_target_pairs={{0,1},{1,2},{4,5},{5,6},{8,9},{9,10},{12,13},{13,14},{16,17},{17,1... | collective-permute-start | bytes 294920 | tf_op jit(solution)/shard_map/ppermute | solution.py:381
  23.0 10.4 %collective-permute-start.4 = (f32[96,256]{1,0:T(8,128)S(1)}, f32[96,256]{1,0:T(8,128)S(1)}, u32[]{:S(2)}, u32[]{:S(2)}) collective-permute-start(f32[96,256]{1,0:T(8,128)S(1)} %get-tuple-element.95), channel_id=1, source_target_pairs={{3,4},{7,8},{11,12},{15,16},{19,20},{23,24},{27,28},{31,0},{35,36}... | collective-permute-start | bytes 294920 | tf_op jit(solution)/shard_map/ppermute | solution.py:381
  34.4 4.5 %collective-permute-start.6 = (f32[96,256]{1,0:T(8,128)S(1)}, f32[96,256]{1,0:T(8,128)S(1)}, u32[]{:S(2)}, u32[]{:S(2)}) collective-permute-start(f32[96,256]{1,0:T(8,128)S(1)} %get-tuple-element.104), channel_id=1, source_target_pairs={{0,1},{1,2},{2,3},{4,5},{5,6},{6,7},{8,9},{9,10},{10,11},{12,13},{... | collective-permute-start | bytes 294920 | tf_op jit(solution)/shard_map/ppermute | solution.py:381
  35.7 10.5 %collective-permute-start.3 = (f32[96,256]{1,0:T(8,128)S(1)}, f32[96,256]{1,0:T(8,128)S(1)}, u32[]{:S(2)}, u32[]{:S(2)}) collective-permute-start(f32[96,256]{1,0:T(8,128)S(1)} %get-tuple-element.94), channel_id=1, source_target_pairs={{3,4},{7,8},{11,12},{15,16},{19,20},{23,24},{27,28},{31,0},{35,36}... | collective-permute-start | bytes 294920 | tf_op jit(solution)/shard_map/ppermute | solution.py:381
  37.0 20.2 %copy-start.1 = (s32[16]{0:T(128)S(1)}, s32[16]{0:T(128)}, u32[]{:S(2)}) copy-start(s32[16]{0:T(128)} %matching.1) | copy-start | bytes 196
  58.6 12.0 %all-to-all-start = ((f32[4,96,256]{2,1,0:T(8,128)}), f32[4,96,256]{2,1,0:T(8,128)S(1)}, u32[]{:S(2)}, u32[]{:S(2)}) async-start(f32[4,96,256]{2,1,0:T(8,128)} %get-tuple-element.113), calls=%async_computation | async-start | bytes 786432 | tf_op jit(solution)/shard_map/all_to_all | solution.py:411
  71.5 4.1 %collective-permute-start.8 = (f32[96,256]{1,0:T(8,128)S(1)}, f32[96,256]{1,0:T(8,128)S(1)}, u32[]{:S(2)}, u32[]{:S(2)}) collective-permute-start(f32[96,256]{1,0:T(8,128)S(1)} %get-tuple-element.123), channel_id=1, source_target_pairs={{0,1},{4,5},{8,9},{12,13},{16,17},{20,21},{24,25},{28,29},{32,33},... | collective-permute-start | bytes 294920 | tf_op jit(solution)/shard_map/ppermute | solution.py:381
  72.8 10.4 %collective-permute-start.7 = (f32[96,256]{1,0:T(8,128)S(1)}, f32[96,256]{1,0:T(8,128)S(1)}, u32[]{:S(2)}, u32[]{:S(2)}) collective-permute-start(f32[96,256]{1,0:T(8,128)S(1)} %get-tuple-element.119), channel_id=1, source_target_pairs={{1,2},{2,3},{3,4},{5,6},{6,7},{7,8},{9,10},{10,11},{11,12},{13,14}... | collective-permute-start | bytes 294920 | tf_op jit(solution)/shard_map/ppermute | solution.py:381
